TPU v7x, 32 devices: a whole 2x2x4 slice. The times are simulated.
32 devices in a mesh: table: 8 (over z, y), col: 4 (over x, core).
Axes of the slice: x: 2, y: 2, z: 4, core: 2. Of those that a mesh axis runs over, the one named last changes fastest.
Arguments:
- embedding: bfloat16 [32768, 256], P('table', 'col'), may hold values from -4 to 4
- accumulator: float32 [32768, 256], P('table', 'col'), may hold values from 0.01 to 1
- pair_rows: int32 [256, 128, 4], P(('table', 'col')), may hold values from 0 to 1023
- pair_len: int32 [256, 128], P(('table', 'col')), may hold values from 0 to 4
- pair_dest: int32 [32, 8], P(('table', 'col')), may hold values from 0 to 7, each once within a row
- pair_tile: int32 [32, 8], P(('table', 'col')), may hold values from 0 to 15
- pooled_grad: bfloat16 [65536, 256], P(('table', 'col')), may hold values from -6 to 6
Outputs:
- pooled: bfloat16 [65536, 256], P(('table', 'col'))
- new_embedding: bfloat16 [32768, 256], P(('table', 'col'))
- new_accumulator: float32 [32768, 256], P(('table', 'col'))
Inputs may be any that keep to these rules, and one draw needn't show every extreme that they name: `pair_dest`: each row names every table index exactly once.
All inputs are finite; a program needn't handle non-finite values.
Results may differ from a plain program's by a relative error of at most 0.0049.
Values may be sent and summed in bfloat16 or wider, within the bound.
No kernel may reach another device: no remote copies, remote signals or barrier semaphores. Data moves between devices by JAX's collectives and lax.ppermute only.
A program may use at most 128 MiB of HBM per device.

v0:
```python
import functools

import jax
import jax.numpy as jnp
from jax import lax
from jax.experimental import pallas as pl
from jax.experimental.pallas import tpu as pltpu
from jax.sharding import PartitionSpec as P


LEARN_RATE = 0.3
EPSILON = 1e-08
MARK_ROWS = 8

ANY = pl.BlockSpec(memory_space=pl.ANY)
HBM = pl.BlockSpec(memory_space=pltpu.HBM)
VMEM = pl.BlockSpec(memory_space=pltpu.VMEM)
SMEM = pl.BlockSpec(memory_space=pltpu.SMEM)


def even(n):
    return n & (n - 1) == 0


def target(i, k, n):
    return i ^ k if even(n) else (i + k) % n


def origin(i, k, n):
    return i ^ k if even(n) else (i + n - k) % n


def step_of(j, i, n):
    return j ^ i if even(n) else lax.rem(j + n - i, n)


def steps(n):
    return sorted(range(1, n), key=lambda k: (-k.bit_length(), k))


def pairs_of(k, n):
    return [(i, target(i, k, n)) for i in range(n)]


def back_of(k, n):
    return [(j, i) for i, j in pairs_of(k, n)]


def call(body, out_shape, in_specs, out_specs, args, scratch=(), limit=None, flops=0):
    size = sum(a.size * a.dtype.itemsize for a in args)
    return pl.pallas_call(
        body,
        out_shape=out_shape,
        in_specs=in_specs,
        out_specs=out_specs,
        scratch_shapes=scratch,
        compiler_params=pltpu.CompilerParams(vmem_limit_bytes=limit),
        cost_estimate=pl.CostEstimate(flops=flops, bytes_accessed=size, transcendentals=0),
    )(*args)


def far(x):
    return pltpu.with_memory_space_constraint(x, pltpu.HBM)


def sequence(n):
    top = [k for k in range(1, n) if 2 * k >= n]
    low = [k for k in range(1, n) if 2 * k < n]
    mixed = []
    while top or low:
        mixed += top[:1] + low[:1]
        top, low = top[1:], low[1:]
    return [("part", k) for k in mixed] + [("cot", k) for k in mixed]


def split_body(count, rows, wide_ref, *refs):
    outs, sems = refs[:count], refs[count]
    me = lax.axis_index("col")
    copies = []
    for k in range(count):
        start = pl.multiple_of(target(me, k, count) * rows, rows)
        copies.append(pltpu.make_async_copy(wide_ref.at[:, pl.ds(start, rows)], outs[k], sems.at[k]))
        copies[k].start()
    for copy in copies:
        copy.wait()


def count_body(cols, wide_ref, rows_hbm, lens_hbm, counts_ref, *refs):
    outs = refs[:cols]
    rows_ref, lens_ref, slab_ref, sems = refs[cols:]
    pairs, looks, bags = rows_ref.shape
    width = counts_ref.shape[0]
    me = lax.axis_index("col")
    rows_copy = pltpu.make_async_copy(rows_hbm, rows_ref, sems.at[cols])
    lens_copy = pltpu.make_async_copy(lens_hbm, lens_ref, sems.at[cols + 1])
    rows_copy.start()
    lens_copy.start()
    copies = []
    for k in range(cols):
        start = pl.multiple_of(target(me, k, cols) * width, width)
        copies.append(
            pltpu.make_async_copy(wide_ref.at[:, pl.ds(start, width)], slab_ref.at[k], sems.at[k])
        )
        copies[k].start()
    rows_copy.wait()
    lens_copy.wait()

    def one(p, carry):
        line = lax.broadcasted_iota(jnp.int32, (width, bags), 0)
        lens = lens_ref[pl.ds(p, 1), :]
        total = jnp.zeros((width, bags), jnp.float32)
        for look in range(looks):
            row = rows_ref[p, pl.ds(look, 1), :]
            row = jnp.where(lens > look, row, -1)
            total = total + (line == row).astype(jnp.float32)
        counts_ref[:, pl.ds(pl.multiple_of(p * bags, bags), bags)] = total.astype(jnp.bfloat16)
        return carry

    lax.fori_loop(0, pairs, one, 0)
    for k in range(cols):
        copies[k].wait()
        outs[k][...] = slab_ref[k].astype(jnp.bfloat16)


def pool_body(tables, cols, span, plan_ref, counts_ref, *refs):
    slabs, outs = refs[:cols], refs[cols : cols + tables]
    wide_ref, parts_ref, pair_ref = refs[cols + tables :]
    thin = slabs[0].shape[0]
    bags = parts_ref.shape[1]
    width = wide_ref.shape[0]
    pairs = plan_ref.shape[1]
    me = lax.axis_index("table")
    for p in range(pairs):
        pair_ref[step_of(plan_ref[0, p], me, tables)] = p
    here = lax.axis_index("col")
    for k in range(cols):
        first = pl.multiple_of(origin(here, k, cols) * thin, thin)
        wide_ref[pl.ds(first, thin), :] = slabs[k][...]
    wide = wide_ref[...]

    def group(g, carry):
        first = pl.multiple_of(g * span * bags, span * bags)
        part = jnp.dot(
            wide, counts_ref[:, pl.ds(first, span * bags)], preferred_element_type=jnp.float32
        )
        for s in range(span):
            parts_ref[g * span + s] = part[:, s * bags : (s + 1) * bags].T.astype(jnp.bfloat16)
        return carry

    lax.fori_loop(0, pairs // span, group, 0)
    outs[0][...] = parts_ref[pair_ref[0]]
    lane = lax.broadcasted_iota(jnp.int32, (MARK_ROWS, width), 1)
    half = width // 2
    for k in range(1, tables):
        p = pair_ref[k]
        tile = plan_ref[1, p]
        outs[k][:bags, :] = parts_ref[p]
        mark = jnp.where(lane < half, tile % 128, tile // 128)
        outs[k][bags:, :] = mark.astype(jnp.float32).astype(jnp.bfloat16)


def read_mark(mark_ref):
    mark = mark_ref[...].astype(jnp.float32)
    half = mark.shape[1] // 2
    low = jnp.max(mark[:, :half]).astype(jnp.int32)
    high = jnp.max(mark[:, half:]).astype(jnp.int32)
    return high * 128 + low


def pick_body(count, bags, *refs):
    marks, grad_ref, outs = refs[:count], refs[count], refs[count + 1 :]
    for k in range(count):
        tile = read_mark(marks[k].at[pl.ds(bags, MARK_ROWS)])
        outs[k][...] = grad_ref[pl.ds(pl.multiple_of(tile * bags, bags), bags), :]


def own_tile(plan_ref):
    tile, me = 0, lax.axis_index("table")
    for p in range(plan_ref.shape[1]):
        tile = jnp.where(plan_ref[0, p] == me, plan_ref[1, p], tile)
    return tile


def sum_body(tables, plan_ref, own_ref, *refs):
    blocks, out_ref, total_ref = refs[: tables - 1], refs[tables - 1], refs[tables]
    bags = own_ref.shape[0]
    total_ref[...] = jnp.zeros_like(total_ref)

    def add(tile, block):
        where = pl.ds(pl.multiple_of(tile * bags, bags), bags)
        total_ref[where, :] += block.astype(jnp.float32)

    add(own_tile(plan_ref), own_ref[...])
    for block_ref in blocks:
        tile = read_mark(block_ref.at[pl.ds(bags, MARK_ROWS)])
        add(tile, block_ref[:bags, :])
    out_ref[...] = total_ref[...].astype(jnp.bfloat16)


def turn_body(cols, *refs):
    slabs, states = refs[:cols], refs[cols : 2 * cols]
    rows_ref, state_ref, wide_ref = refs[2 * cols :]
    thin = slabs[0].shape[0]
    here = lax.axis_index("col")
    for source, out_ref in ((slabs, rows_ref), (states, state_ref)):
        for k in range(cols):
            first = pl.multiple_of(origin(here, k, cols) * thin, thin)
            wide_ref[pl.ds(first, thin), :] = source[k][...].astype(jnp.float32)
        out_ref[...] = wide_ref[...].T.astype(out_ref.dtype)


def update_body(tables, chunk, plan_ref, grad_ref, counts_ref, rows_ref, state_ref, *refs):
    blocks = refs[: tables - 1]
    out_rows_ref, out_state_ref, new_rows_ref, new_state_ref, cots_ref, pair_ref, sems = refs[tables - 1 :]
    bags = blocks[0].shape[0]
    me = lax.axis_index("table")
    for p in range(plan_ref.shape[1]):
        pair_ref[step_of(plan_ref[0, p], me, tables)] = p

    def put(k, block):
        first = pl.multiple_of(pair_ref[k] * bags, bags)
        cots_ref[pl.ds(first, bags), :] = block

    tile = own_tile(plan_ref)
    put(0, grad_ref[pl.ds(pl.multiple_of(tile * bags, bags), bags), :])
    for k in range(1, tables):
        put(k, blocks[k - 1][...])

    copies = []
    for r in range(counts_ref.shape[0] // chunk):
        where = pl.ds(r * chunk, chunk)
        grad = jnp.dot(counts_ref[where, :], cots_ref[...], preferred_element_type=jnp.float32)
        state = state_ref[where, :].astype(jnp.float32) + grad * grad
        rows = rows_ref[where, :].astype(jnp.float32)
        new_state_ref[where, :] = state
        new_rows_ref[where, :] = (
            rows - LEARN_RATE * grad / (jnp.sqrt(state) + EPSILON)
        ).astype(jnp.bfloat16)
        for i, (src, dst) in enumerate(((new_state_ref, out_state_ref), (new_rows_ref, out_rows_ref))):
            copy = pltpu.make_async_copy(src.at[where], dst.at[where], sems.at[r, i])
            copy.start()
            copies.append(copy)
    for copy in copies:
        copy.wait()


def per_device(embedding, accumulator, pair_rows, pair_len, pair_dest, pair_tile, pooled_grad):
    tables, cols = lax.axis_size("table"), lax.axis_size("col")
    pairs, bags, looks = pair_rows.shape
    thin = embedding.shape[1]
    width = thin * cols
    rows = embedding.shape[0] // cols
    span = min(8, pairs)
    chunk = min(256, rows)
    shape, near = jax.ShapeDtypeStruct, pltpu.VMEM
    bf16 = jnp.bfloat16
    mega = 1 << 20
    spare = pairs * bags * width * 2
    big = 4 * mega + rows * pairs * bags * 2 + 4 * spare + 12 * rows * width

    plan = jnp.concatenate([pair_dest, pair_tile])

    def over_col(parts):
        moved = {k: lax.ppermute(parts[k], "col", pairs_of(k, cols)) for k in steps(cols)}
        return [parts[0]] + [moved[k] for k in range(1, cols)]

    slabs = call(
        functools.partial(split_body, cols, rows),
        [near((thin, rows), bf16)] * cols,
        [HBM],
        [VMEM] * cols,
        (far(embedding.T),),
        scratch=[pltpu.SemaphoreType.DMA((cols,))],
        limit=8 * mega,
    )
    slabs = over_col(slabs)
    counts, *states = call(
        functools.partial(count_body, cols),
        [near((rows, pairs * bags), bf16)] + [near((thin, rows), bf16)] * cols,
        [HBM, HBM, HBM],
        [VMEM] * (1 + cols),
        (far(accumulator.T), far(jnp.transpose(pair_rows, (0, 2, 1))), far(pair_len)),
        scratch=[
            pltpu.VMEM((pairs, looks, bags), jnp.int32),
            pltpu.VMEM((pairs, bags), jnp.int32),
            pltpu.VMEM((cols, thin, rows), jnp.float32),
            pltpu.SemaphoreType.DMA((cols + 2,)),
        ],
        limit=8 * mega + rows * pairs * bags * 2,
    )
    states = over_col(states)

    sent = call(
        functools.partial(pool_body, tables, cols, span),
        [near((bags, width), bf16)] + [near((bags + MARK_ROWS, width), bf16)] * (tables - 1),
        [SMEM, VMEM] + [VMEM] * cols,
        [VMEM] * tables,
        (plan, counts, *slabs),
        scratch=[
            pltpu.VMEM((width, rows), bf16),
            pltpu.VMEM((pairs, bags, width), bf16),
            pltpu.SMEM((pairs,), jnp.int32),
        ],
        limit=big,
        flops=2 * rows * width * pairs * bags,
    )
    own_block = sent[0]
    arrived, returned = {}, {}
    for kind, k in sequence(tables):
        if kind == "part":
            arrived[k] = lax.ppermute(sent[k], "table", pairs_of(k, tables))
        else:
            picked = call(
                functools.partial(pick_body, 1, bags),
                [near((bags, width), bf16)],
                [VMEM, VMEM],
                [VMEM],
                (arrived[k], pooled_grad),
                limit=8 * mega + 2 * spare,
            )
            returned[k] = lax.ppermute(picked[0], "table", back_of(k, tables))

    pooled = call(
        functools.partial(sum_body, tables),
        shape(pooled_grad.shape, bf16),
        [SMEM, VMEM] + [VMEM] * (tables - 1),
        VMEM,
        (plan, own_block, *[arrived[k] for k in range(1, tables)]),
        scratch=[pltpu.VMEM(pooled_grad.shape, jnp.float32)],
        limit=8 * mega + 2 * spare,
    )

    turned = call(
        functools.partial(turn_body, cols),
        [near((rows, width), bf16), near((rows, width), bf16)],
        [VMEM] * (2 * cols),
        [VMEM, VMEM],
        (*slabs, *states),
        scratch=[pltpu.VMEM((width, rows), jnp.float32)],
        limit=16 * mega,
    )
    new_rows, new_state = call(
        functools.partial(update_body, tables, chunk),
        [shape((rows, width), bf16), shape((rows, width), jnp.float32)],
        [SMEM, VMEM, VMEM, VMEM, VMEM] + [VMEM] * (tables - 1),
        [ANY, ANY],
        (plan, pooled_grad, counts, *turned, *[returned[k] for k in range(1, tables)]),
        scratch=[
            pltpu.VMEM((rows, width), bf16),
            pltpu.VMEM((rows, width), jnp.float32),
            pltpu.VMEM((pairs * bags, width), bf16),
            pltpu.SMEM((pairs,), jnp.int32),
            pltpu.SemaphoreType.DMA((rows // chunk, 2)),
        ],
        limit=big,
        flops=2 * rows * width * pairs * bags,
    )
    return (pooled, new_rows, new_state)


def solution(mesh):
    return jax.shard_map(
        per_device,
        mesh=mesh,
        in_specs=(
            P("table", "col"),
            P("table", "col"),
            P(("table", "col"), None, None),
            P(("table", "col"), None),
            P(("table", "col"), None),
            P(("table", "col"), None),
            P(("table", "col"), None),
        ),
        out_specs=(P(("table", "col"), None), P(("table", "col"), None), P(("table", "col"), None)),
        check_vma=False,
    )
```

profile of v0, /device:TPU:0, one launch (start us, length us, event | category | flops | bytes accessed | tf_op | source)
XLA Modules:
  0.0 51.0 jit_solution(15173349316639208544)
XLA Ops:
  0.6 1.2 %shard_map.95 = (bf16[64,1024]{1,0:T(8,128)(2,1)S(1)}, bf16[64,1024]{1,0:T(8,128)(2,1)S(1)}, bf16[64,1024]{1,0:T(8,128)(2,1)S(1)}, bf16[64,1024]{1,0:T(8,128)(2,1)S(1)}) custom-call(bf16[64,4096]{1,0:T(8,128)(2,1)} %bitcast.4), custom_call_target="tpu_custom_call" | custom-call | bytes 524288 | tf_op jit(solution)/shard_map/pallas_call | solution.py:51
  1.9 0.6 %collective-permute-start = (bf16[64,1024]{1,0:T(8,128)(2,1)S(1)}, bf16[64,1024]{1,0:T(8,128)(2,1)S(1)}, u32[]{:S(2)}, u32[]{:S(2)}) collective-permute-start(bf16[64,1024]{1,0:T(8,128)(2,1)S(1)} %get-tuple-element.26), channel_id=1, source_target_pairs={{0,1},{1,0},{2,3},{3,2},{4,5},{5,4},{6,7},{7,6},{8,9},{9,8},{10,11... | collective-permute-start | bytes 393224 | tf_op jit(solution)/shard_map/ppermute | solution.py:264
  2.4 2.6 %collective-permute-start.1 = (bf16[64,1024]{1,0:T(8,128)(2,1)S(1)}, bf16[64,1024]{1,0:T(8,128)(2,1)S(1)}, u32[]{:S(2)}, u32[]{:S(2)}) collective-permute-start(bf16[64,1024]{1,0:T(8,128)(2,1)S(1)} %get-tuple-element.27), channel_id=1, source_target_pairs={{0,2},{1,3},{2,0},{3,1},{4,6},{5,7},{6,4},{7,5},{8,10},{9,11},{10,... | collective-permute-start | bytes 393224 | tf_op jit(solution)/shard_map/ppermute | solution.py:264
  5.0 2.6 %shard_map.94 = (bf16[1024,1024]{1,0:T(8,128)(2,1)S(1)}, bf16[64,1024]{1,0:T(8,128)(2,1)S(1)}, bf16[64,1024]{1,0:T(8,128)(2,1)S(1)}, bf16[64,1024]{1,0:T(8,128)(2,1)S(1)}, bf16[64,1024]{1,0:T(8,128)(2,1)S(1)}) custom-call(f32[64,4096]{1,0:T(8,128)} %bitcast.3, s32[8,4,128]{2,1,0:T(4,128)} %bitcast.5, s32[8,128]{1,0:T(8,128)} %lens_hbm.1), custom_call_target="tpu_custom_call" | custom-call | bytes 1069056 | tf_op jit(solution)/shard_map/pallas_call | solution.py:51
  7.7 0.7 %pad_add_fusion.plan_ref = s32[2,8]{1,0:T(2,128)S(1)} fusion(s32[1,8]{1,0:T(1,128)} %param.12, s32[1,8]{1,0:T(1,128)} %param.11), kind=kLoop, calls=%fused_computation | loop fusion | flops 16 | bytes 128 | tf_op jit(solution)/shard_map/concatenate | solution.py:261
  8.4 1.0 %collective-permute-done.1.refs_2_ = bf16[64,1024]{1,0:T(8,128)(2,1)S(1)} collective-permute-done((bf16[64,1024]{1,0:T(8,128)(2,1)S(1)}, bf16[64,1024]{1,0:T(8,128)(2,1)S(1)}, u32[]{:S(2)}, u32[]{:S(2)}) %collective-permute-start.1) | collective-permute-done | bytes 131104 | tf_op jit(solution)/shard_map/ppermute | solution.py:264
  9.3 2.3 %collective-permute-done.2.refs_3_ = bf16[64,1024]{1,0:T(8,128)(2,1)S(1)} collective-permute-done((bf16[64,1024]{1,0:T(8,128)(2,1)S(1)}, bf16[64,1024]{1,0:T(8,128)(2,1)S(1)}, u32[]{:S(2)}, u32[]{:S(2)}) %collective-permute-start.2) | collective-permute-done | bytes 131104 | tf_op jit(solution)/shard_map/ppermute | solution.py:264
  11.6 1.4 %shard_map.96 = (bf16[128,256]{1,0:T(8,128)(2,1)S(1)}, bf16[136,256]{1,0:T(8,128)(2,1)S(1)}, bf16[136,256]{1,0:T(8,128)(2,1)S(1)}, bf16[136,256]{1,0:T(8,128)(2,...) custom-call(s32[2,8]{1,0:T(2,128)S(1)} %pad_add_fusion.plan_ref, ...), custom_call_target="tpu_custom_call" | custom-call | flops 536870912 | bytes 2621504 | tf_op jit(solution)/shard_map/pallas_call | solution.py:51
  13.0 1.6 %collective-permute-start.3 = (bf16[136,256]{1,0:T(8,128)(2,1)S(1)}, bf16[136,256]{1,0:T(8,128)(2,1)S(1)}, u32[]{:S(2)}, u32[]{:S(2)}) collective-permute-start(bf16[136,256]{1,0:T(8,128)(2,1)S(1)} %get-tuple-element.30), channel_id=1, source_target_pairs={{0,4},{4,0},{8,12},{12,8},{16,20},{20,16},{24,28},{28,24},{1,5},{5... | collective-permute-start | bytes 208904 | tf_op jit(solution)/shard_map/ppermute | solution.py:311
  14.6 1.6 %collective-permute-start.4 = (bf16[136,256]{1,0:T(8,128)(2,1)S(1)}, bf16[136,256]{1,0:T(8,128)(2,1)S(1)}, u32[]{:S(2)}, u32[]{:S(2)}) collective-permute-start(bf16[136,256]{1,0:T(8,128)(2,1)S(1)} %get-tuple-element.31), channel_id=1, source_target_pairs={{0,8},{4,12},{8,0},{12,4},{16,24},{20,28},{24,16},{28,20},{1,9},{5... | collective-permute-start | bytes 208904 | tf_op jit(solution)/shard_map/ppermute | solution.py:311
  16.2 0.4 collective-permute-start.5
  16.6 2.6 %collective-permute-start.6 = (bf16[136,256]{1,0:T(8,128)(2,1)S(1)}, bf16[136,256]{1,0:T(8,128)(2,1)S(1)}, u32[]{:S(2)}, u32[]{:S(2)}) collective-permute-start(bf16[136,256]{1,0:T(8,128)(2,1)S(1)} %get-tuple-element.33), channel_id=1, source_target_pairs={{0,16},{4,20},{8,24},{12,28},{16,0},{20,4},{24,8},{28,12},{1,17},{... | collective-permute-start | bytes 208904 | tf_op jit(solution)/shard_map/ppermute | solution.py:311
  19.2 1.3 %collective-permute-start.7 = (bf16[136,256]{1,0:T(8,128)(2,1)S(1)}, bf16[136,256]{1,0:T(8,128)(2,1)S(1)}, u32[]{:S(2)}, u32[]{:S(2)}) collective-permute-start(bf16[136,256]{1,0:T(8,128)(2,1)S(1)} %get-tuple-element.34), channel_id=1, source_target_pairs={{0,20},{4,16},{8,28},{12,24},{16,4},{20,0},{24,12},{28,8},{1,21},{... | collective-permute-start | bytes 208904 | tf_op jit(solution)/shard_map/ppermute | solution.py:311
  20.5 3.6 %collective-permute-start.8 = (bf16[136,256]{1,0:T(8,128)(2,1)S(1)}, bf16[136,256]{1,0:T(8,128)(2,1)S(1)}, u32[]{:S(2)}, u32[]{:S(2)}) collective-permute-start(bf16[136,256]{1,0:T(8,128)(2,1)S(1)} %get-tuple-element.35), channel_id=1, source_target_pairs={{0,24},{4,28},{8,16},{12,20},{16,8},{20,12},{24,0},{28,4},{1,25},{... | collective-permute-start | bytes 208904 | tf_op jit(solution)/shard_map/ppermute | solution.py:311
  24.1 0.2 collective-permute-start.9
  24.3 1.5 %collective-permute-start.11 = (bf16[64,1024]{1,0:T(8,128)(2,1)S(1)}, bf16[64,1024]{1,0:T(8,128)(2,1)S(1)}, u32[]{:S(2)}, u32[]{:S(2)}) collective-permute-start(bf16[64,1024]{1,0:T(8,128)(2,1)S(1)} %get-tuple-element.39), channel_id=1, source_target_pairs={{0,2},{1,3},{2,0},{3,1},{4,6},{5,7},{6,4},{7,5},{8,10},{9,11},{10,... | collective-permute-start | bytes 393224 | tf_op jit(solution)/shard_map/ppermute | solution.py:264
  25.8 4.0 %collective-permute-done.7.refs_4_.refs_0_ = bf16[136,256]{1,0:T(8,128)(2,1)S(1)} collective-permute-done((bf16[136,256]{1,0:T(8,128)(2,1)S(1)}, bf16[136,256]{1,0:T(8,128)(2,1)S(1)}, u32[]{:S(2)}, u32[]{:S(2)}) %collective-permute-start.7) | collective-permute-done | bytes 69664 | tf_op jit(solution)/shard_map/ppermute | solution.py:311
  29.8 0.4 collective-permute-start.12
  30.4 0.1 shard_map.100
  30.6 1.3 %collective-permute-start.13 = (bf16[128,256]{1,0:T(8,128)(2,1)S(1)}, bf16[128,256]{1,0:T(8,128)(2,1)S(1)}, u32[]{:S(2)}, u32[]{:S(2)}) collective-permute-start(bf16[128,256]{1,0:T(8,128)(2,1)S(1)} %shard_map.99), channel_id=1, source_target_pairs={{4,0},{0,4},{12,8},{8,12},{20,16},{16,20},{28,24},{24,28},{5,1},{1... | collective-permute-start | bytes 196616 | tf_op jit(solution)/shard_map/ppermute | solution.py:321
  31.8 1.9 %collective-permute-start.14 = (bf16[128,256]{1,0:T(8,128)(2,1)S(1)}, bf16[128,256]{1,0:T(8,128)(2,1)S(1)}, u32[]{:S(2)}, u32[]{:S(2)}) collective-permute-start(bf16[128,256]{1,0:T(8,128)(2,1)S(1)} %shard_map.100), channel_id=1, source_target_pairs={{8,0},{12,4},{0,8},{4,12},{24,16},{28,20},{16,24},{20,28},{9,1},{1... | collective-permute-start | bytes 196616 | tf_op jit(solution)/shard_map/ppermute | solution.py:321
  33.9 0.1 shard_map.102
  34.0 0.1 shard_map.103
  34.4 0.5 collective-permute-start.15
  34.9 2.9 %collective-permute-start.16 = (bf16[128,256]{1,0:T(8,128)(2,1)S(1)}, bf16[128,256]{1,0:T(8,128)(2,1)S(1)}, u32[]{:S(2)}, u32[]{:S(2)}) collective-permute-start(bf16[128,256]{1,0:T(8,128)(2,1)S(1)} %shard_map.102), channel_id=1, source_target_pairs={{16,0},{20,4},{24,8},{28,12},{0,16},{4,20},{8,24},{12,28},{17,1},{... | collective-permute-start | bytes 196616 | tf_op jit(solution)/shard_map/ppermute | solution.py:321
  37.9 1.0 %collective-permute-start.17 = (bf16[128,256]{1,0:T(8,128)(2,1)S(1)}, bf16[128,256]{1,0:T(8,128)(2,1)S(1)}, u32[]{:S(2)}, u32[]{:S(2)}) collective-permute-start(bf16[128,256]{1,0:T(8,128)(2,1)S(1)} %shard_map.103), channel_id=1, source_target_pairs={{20,0},{16,4},{28,8},{24,12},{4,16},{0,20},{12,24},{8,28},{21,1},{... | collective-permute-start | bytes 196616 | tf_op jit(solution)/shard_map/ppermute | solution.py:321
  38.8 2.3 %collective-permute-start.18 = (bf16[128,256]{1,0:T(8,128)(2,1)S(1)}, bf16[128,256]{1,0:T(8,128)(2,1)S(1)}, u32[]{:S(2)}, u32[]{:S(2)}) collective-permute-start(bf16[128,256]{1,0:T(8,128)(2,1)S(1)} %shard_map.104), channel_id=1, source_target_pairs={{24,0},{28,4},{16,8},{20,12},{8,16},{12,20},{0,24},{4,28},{25,1},{... | collective-permute-start | bytes 196616 | tf_op jit(solution)/shard_map/ppermute | solution.py:321
  41.2 1.5 %collective-permute-start.19 = (bf16[128,256]{1,0:T(8,128)(2,1)S(1)}, bf16[128,256]{1,0:T(8,128)(2,1)S(1)}, u32[]{:S(2)}, u32[]{:S(2)}) collective-permute-start(bf16[128,256]{1,0:T(8,128)(2,1)S(1)} %shard_map.105), channel_id=1, source_target_pairs={{28,0},{24,4},{20,8},{16,12},{12,16},{8,20},{4,24},{0,28},{29,1},{... | collective-permute-start | bytes 196616 | tf_op jit(solution)/shard_map/ppermute | solution.py:321
  42.7 0.5 shard_map.98
  43.1 1.9 %shard_map.97 = bf16[2048,256]{1,0:T(8,128)(2,1)} custom-call(s32[2,8]{1,0:T(2,128)S(1)} %pad_add_fusion.plan_ref, bf16[128,256]{1,0:T(8,128)(2,1)S(1)} %get-tuple-element.29.own_ref, bf16[136,256]{1,0:T(8,128)(2,1)S(1)} %collective-permute-done.3.refs_0_, bf16[136,256]{1,0:T(8,128)(2,1)S(1)} %collective-permute-done.4.refs_1_.refs_0_, ...), custom_call_target="tpu_custom_call" | custom-call | bytes 553024 | tf_op jit(solution)/shard_map/pallas_call | solution.py:51
  45.0 3.2 %collective-permute-done.17.refs_4_ = bf16[128,256]{1,0:T(8,128)(2,1)S(1)} collective-permute-done((bf16[128,256]{1,0:T(8,128)(2,1)S(1)}, bf16[128,256]{1,0:T(8,128)(2,1)S(1)}, u32[]{:S(2)}, u32[]{:S(2)}) %collective-permute-start.17) | collective-permute-done | bytes 65568 | tf_op jit(solution)/shard_map/ppermute | solution.py:321
  48.3 2.7 %shard_map.106 = (bf16[1024,256]{1,0:T(8,128)(2,1)}, f32[1024,256]{1,0:T(8,128)}) custom-call(s32[2,8]{1,0:T(2,128)S(1)} %pad_add_fusion.plan_ref, bf16[2048,256]{1,0:T(8,128)(2,1)S(1)} %copy-done, bf16[1024,1024]{1,0:T(8,128)(2,1)S(1)} %get-tuple-element.24.counts_ref, bf16[1024,256]{1,0:T(8,128)(2,1)S(1)} %get-tuple-element.41.rows_ref, ...), custom_call_target="tpu_custom_call" | custom-call | flops 536870912 | bytes 4653120 | tf_op jit(solution)/shard_map/pallas_call | solution.py:51
  (24 shorter events, 0.6 us)
Async XLA Ops:
  0.6 29.6 %copy-start = (bf16[2048,256]{1,0:T(8,128)(2,1)S(1)}, bf16[2048,256]{1,0:T(8,128)(2,1)}, u32[]{:S(2)}) copy-start(bf16[2048,256]{1,0:T(8,128)(2,1)} %grad_ref.1) | copy-start | bytes 3145732
  1.9 6.5 %collective-permute-start = (bf16[64,1024]{1,0:T(8,128)(2,1)S(1)}, bf16[64,1024]{1,0:T(8,128)(2,1)S(1)}, u32[]{:S(2)}, u32[]{:S(2)}) collective-permute-start(bf16[64,1024]{1,0:T(8,128)(2,1)S(1)} %get-tuple-element.26), channel_id=1, source_target_pairs={{0,1},{1,0},{2,3},{3,2},{4,5},{5,4},{6,7},{7,6},{8,9},{9,8},{10,11... | collective-permute-start | bytes 393224 | tf_op jit(solution)/shard_map/ppermute | solution.py:264
  2.4 6.9 %collective-permute-start.1 = (bf16[64,1024]{1,0:T(8,128)(2,1)S(1)}, bf16[64,1024]{1,0:T(8,128)(2,1)S(1)}, u32[]{:S(2)}, u32[]{:S(2)}) collective-permute-start(bf16[64,1024]{1,0:T(8,128)(2,1)S(1)} %get-tuple-element.27), channel_id=1, source_target_pairs={{0,2},{1,3},{2,0},{3,1},{4,6},{5,7},{6,4},{7,5},{8,10},{9,11},{10,... | collective-permute-start | bytes 393224 | tf_op jit(solution)/shard_map/ppermute | solution.py:264
  5.0 6.6 %collective-permute-start.2 = (bf16[64,1024]{1,0:T(8,128)(2,1)S(1)}, bf16[64,1024]{1,0:T(8,128)(2,1)S(1)}, u32[]{:S(2)}, u32[]{:S(2)}) collective-permute-start(bf16[64,1024]{1,0:T(8,128)(2,1)S(1)} %get-tuple-element.28), channel_id=1, source_target_pairs={{0,3},{1,2},{2,1},{3,0},{4,7},{5,6},{6,5},{7,4},{8,11},{9,10},{10,... | collective-permute-start | bytes 393224 | tf_op jit(solution)/shard_map/ppermute | solution.py:264
  13.0 7.4 %collective-permute-start.3 = (bf16[136,256]{1,0:T(8,128)(2,1)S(1)}, bf16[136,256]{1,0:T(8,128)(2,1)S(1)}, u32[]{:S(2)}, u32[]{:S(2)}) collective-permute-start(bf16[136,256]{1,0:T(8,128)(2,1)S(1)} %get-tuple-element.30), channel_id=1, source_target_pairs={{0,4},{4,0},{8,12},{12,8},{16,20},{20,16},{24,28},{28,24},{1,5},{5... | collective-permute-start | bytes 208904 | tf_op jit(solution)/shard_map/ppermute | solution.py:311
  14.6 9.5 %collective-permute-start.4 = (bf16[136,256]{1,0:T(8,128)(2,1)S(1)}, bf16[136,256]{1,0:T(8,128)(2,1)S(1)}, u32[]{:S(2)}, u32[]{:S(2)}) collective-permute-start(bf16[136,256]{1,0:T(8,128)(2,1)S(1)} %get-tuple-element.31), channel_id=1, source_target_pairs={{0,8},{4,12},{8,0},{12,4},{16,24},{20,28},{24,16},{28,20},{1,9},{5... | collective-permute-start | bytes 208904 | tf_op jit(solution)/shard_map/ppermute | solution.py:311
  16.2 8.1 %collective-permute-start.5 = (bf16[136,256]{1,0:T(8,128)(2,1)S(1)}, bf16[136,256]{1,0:T(8,128)(2,1)S(1)}, u32[]{:S(2)}, u32[]{:S(2)}) collective-permute-start(bf16[136,256]{1,0:T(8,128)(2,1)S(1)} %get-tuple-element.32), channel_id=1, source_target_pairs={{0,12},{4,8},{8,4},{12,0},{16,28},{20,24},{24,20},{28,16},{1,13},{... | collective-permute-start | bytes 208904 | tf_op jit(solution)/shard_map/ppermute | solution.py:311
  16.6 7.7 %collective-permute-start.6 = (bf16[136,256]{1,0:T(8,128)(2,1)S(1)}, bf16[136,256]{1,0:T(8,128)(2,1)S(1)}, u32[]{:S(2)}, u32[]{:S(2)}) collective-permute-start(bf16[136,256]{1,0:T(8,128)(2,1)S(1)} %get-tuple-element.33), channel_id=1, source_target_pairs={{0,16},{4,20},{8,24},{12,28},{16,0},{20,4},{24,8},{28,12},{1,17},{... | collective-permute-start | bytes 208904 | tf_op jit(solution)/shard_map/ppermute | solution.py:311
  19.2 10.7 %collective-permute-start.7 = (bf16[136,256]{1,0:T(8,128)(2,1)S(1)}, bf16[136,256]{1,0:T(8,128)(2,1)S(1)}, u32[]{:S(2)}, u32[]{:S(2)}) collective-permute-start(bf16[136,256]{1,0:T(8,128)(2,1)S(1)} %get-tuple-element.34), channel_id=1, source_target_pairs={{0,20},{4,16},{8,28},{12,24},{16,4},{20,0},{24,12},{28,8},{1,21},{... | collective-permute-start | bytes 208904 | tf_op jit(solution)/shard_map/ppermute | solution.py:311
  20.5 10.1 %collective-permute-start.8 = (bf16[136,256]{1,0:T(8,128)(2,1)S(1)}, bf16[136,256]{1,0:T(8,128)(2,1)S(1)}, u32[]{:S(2)}, u32[]{:S(2)}) collective-permute-start(bf16[136,256]{1,0:T(8,128)(2,1)S(1)} %get-tuple-element.35), channel_id=1, source_target_pairs={{0,24},{4,28},{8,16},{12,20},{16,8},{20,12},{24,0},{28,4},{1,25},{... | collective-permute-start | bytes 208904 | tf_op jit(solution)/shard_map/ppermute | solution.py:311
  24.1 7.8 %collective-permute-start.9 = (bf16[136,256]{1,0:T(8,128)(2,1)S(1)}, bf16[136,256]{1,0:T(8,128)(2,1)S(1)}, u32[]{:S(2)}, u32[]{:S(2)}) collective-permute-start(bf16[136,256]{1,0:T(8,128)(2,1)S(1)} %get-tuple-element.36), channel_id=1, source_target_pairs={{0,28},{4,24},{8,20},{12,16},{16,12},{20,8},{24,4},{28,0},{1,29},{... | collective-permute-start | bytes 208904 | tf_op jit(solution)/shard_map/ppermute | solution.py:311
  24.3 10.2 %collective-permute-start.10 = (bf16[64,1024]{1,0:T(8,128)(2,1)S(1)}, bf16[64,1024]{1,0:T(8,128)(2,1)S(1)}, u32[]{:S(2)}, u32[]{:S(2)}) collective-permute-start(bf16[64,1024]{1,0:T(8,128)(2,1)S(1)} %get-tuple-element.38), channel_id=1, source_target_pairs={{0,1},{1,0},{2,3},{3,2},{4,5},{5,4},{6,7},{7,6},{8,9},{9,8},{10,11... | collective-permute-start | bytes 393224 | tf_op jit(solution)/shard_map/ppermute | solution.py:264
  24.3 10.7 %collective-permute-start.11 = (bf16[64,1024]{1,0:T(8,128)(2,1)S(1)}, bf16[64,1024]{1,0:T(8,128)(2,1)S(1)}, u32[]{:S(2)}, u32[]{:S(2)}) collective-permute-start(bf16[64,1024]{1,0:T(8,128)(2,1)S(1)} %get-tuple-element.39), channel_id=1, source_target_pairs={{0,2},{1,3},{2,0},{3,1},{4,6},{5,7},{6,4},{7,5},{8,10},{9,11},{10,... | collective-permute-start | bytes 393224 | tf_op jit(solution)/shard_map/ppermute | solution.py:264
  29.8 8.0 %collective-permute-start.12 = (bf16[64,1024]{1,0:T(8,128)(2,1)S(1)}, bf16[64,1024]{1,0:T(8,128)(2,1)S(1)}, u32[]{:S(2)}, u32[]{:S(2)}) collective-permute-start(bf16[64,1024]{1,0:T(8,128)(2,1)S(1)} %get-tuple-element.40), channel_id=1, source_target_pairs={{0,3},{1,2},{2,1},{3,0},{4,7},{5,6},{6,5},{7,4},{8,11},{9,10},{10,... | collective-permute-start | bytes 393224 | tf_op jit(solution)/shard_map/ppermute | solution.py:264
  30.6 8.3 %collective-permute-start.13 = (bf16[128,256]{1,0:T(8,128)(2,1)S(1)}, bf16[128,256]{1,0:T(8,128)(2,1)S(1)}, u32[]{:S(2)}, u32[]{:S(2)}) collective-permute-start(bf16[128,256]{1,0:T(8,128)(2,1)S(1)} %shard_map.99), channel_id=1, source_target_pairs={{4,0},{0,4},{12,8},{8,12},{20,16},{16,20},{28,24},{24,28},{5,1},{1... | collective-permute-start | bytes 196616 | tf_op jit(solution)/shard_map/ppermute | solution.py:321
  31.8 9.3 %collective-permute-start.14 = (bf16[128,256]{1,0:T(8,128)(2,1)S(1)}, bf16[128,256]{1,0:T(8,128)(2,1)S(1)}, u32[]{:S(2)}, u32[]{:S(2)}) collective-permute-start(bf16[128,256]{1,0:T(8,128)(2,1)S(1)} %shard_map.100), channel_id=1, source_target_pairs={{8,0},{12,4},{0,8},{4,12},{24,16},{28,20},{16,24},{20,28},{9,1},{1... | collective-permute-start | bytes 196616 | tf_op jit(solution)/shard_map/ppermute | solution.py:321
  34.4 10.6 %collective-permute-start.15 = (bf16[128,256]{1,0:T(8,128)(2,1)S(1)}, bf16[128,256]{1,0:T(8,128)(2,1)S(1)}, u32[]{:S(2)}, u32[]{:S(2)}) collective-permute-start(bf16[128,256]{1,0:T(8,128)(2,1)S(1)} %shard_map.101), channel_id=1, source_target_pairs={{12,0},{8,4},{4,8},{0,12},{28,16},{24,20},{20,24},{16,28},{13,1},{... | collective-permute-start | bytes 196616 | tf_op jit(solution)/shard_map/ppermute | solution.py:321
  34.9 10.1 %collective-permute-start.16 = (bf16[128,256]{1,0:T(8,128)(2,1)S(1)}, bf16[128,256]{1,0:T(8,128)(2,1)S(1)}, u32[]{:S(2)}, u32[]{:S(2)}) collective-permute-start(bf16[128,256]{1,0:T(8,128)(2,1)S(1)} %shard_map.102), channel_id=1, source_target_pairs={{16,0},{20,4},{24,8},{28,12},{0,16},{4,20},{8,24},{12,28},{17,1},{... | collective-permute-start | bytes 196616 | tf_op jit(solution)/shard_map/ppermute | solution.py:321
  37.9 10.4 %collective-permute-start.17 = (bf16[128,256]{1,0:T(8,128)(2,1)S(1)}, bf16[128,256]{1,0:T(8,128)(2,1)S(1)}, u32[]{:S(2)}, u32[]{:S(2)}) collective-permute-start(bf16[128,256]{1,0:T(8,128)(2,1)S(1)} %shard_map.103), channel_id=1, source_target_pairs={{20,0},{16,4},{28,8},{24,12},{4,16},{0,20},{12,24},{8,28},{21,1},{... | collective-permute-start | bytes 196616 | tf_op jit(solution)/shard_map/ppermute | solution.py:321
  38.8 9.4 %collective-permute-start.18 = (bf16[128,256]{1,0:T(8,128)(2,1)S(1)}, bf16[128,256]{1,0:T(8,128)(2,1)S(1)}, u32[]{:S(2)}, u32[]{:S(2)}) collective-permute-start(bf16[128,256]{1,0:T(8,128)(2,1)S(1)} %shard_map.104), channel_id=1, source_target_pairs={{24,0},{28,4},{16,8},{20,12},{8,16},{12,20},{0,24},{4,28},{25,1},{... | collective-permute-start | bytes 196616 | tf_op jit(solution)/shard_map/ppermute | solution.py:321
  41.2 7.1 %collective-permute-start.19 = (bf16[128,256]{1,0:T(8,128)(2,1)S(1)}, bf16[128,256]{1,0:T(8,128)(2,1)S(1)}, u32[]{:S(2)}, u32[]{:S(2)}) collective-permute-start(bf16[128,256]{1,0:T(8,128)(2,1)S(1)} %shard_map.105), channel_id=1, source_target_pairs={{28,0},{24,4},{20,8},{16,12},{12,16},{8,20},{4,24},{0,28},{29,1},{... | collective-permute-start | bytes 196616 | tf_op jit(solution)/shard_map/ppermute | solution.py:321
where the time goes:
time: 51.7 us; the launch traced here: 51 us
  starting transfers between devices  27.7 us (54%)
  Pallas kernels  11.3 us (22%)
  waiting for transfers between devices  10.6 us (21%)
  between operations  0.77 us (1%)
  other arithmetic  0.68 us (1%)
    ppermute x7, starting transfers between devices, per_device(): returned[k] = lax.ppermute(picked[0], 'table', back_of(k, tables))  11.4 us
    pallas_call x13, Pallas kernels, call(): pl.pallas_call(body, out_shape=out_shape, in_specs=in_specs, out_specs=ou...  11.3 us
    ppermute x7, starting transfers between devices, per_device(): arrived[k] = lax.ppermute(sent[k], 'table', pairs_of(k, tables))  11.2 us
    ppermute x6, starting transfers between devices, over_col(): lax.ppermute(parts[k], 'col', pairs_of(k, cols))  5.11 us
    ppermute x7, waiting for transfers between devices, per_device(): arrived[k] = lax.ppermute(sent[k], 'table', pairs_of(k, tables))  4.06 us
    ppermute x6, waiting for transfers between devices, over_col(): lax.ppermute(parts[k], 'col', pairs_of(k, cols))  3.28 us
    ppermute x7, waiting for transfers between devices, per_device(): returned[k] = lax.ppermute(picked[0], 'table', back_of(k, tables))  3.26 us
  transfers between devices with their start and end apart: 20, of which 4 were waited for; matrix products, arithmetic and copies ran while one was open for 1% of the time, Pallas kernels for 12%

commit v1 on v0

v1 whole, which is shorter than its diff:
```python
import functools

import jax
import jax.numpy as jnp
from jax import lax
from jax.experimental import pallas as pl
from jax.experimental.pallas import tpu as pltpu
from jax.sharding import PartitionSpec as P


LEARN_RATE = 0.3
EPSILON = 1e-08
MARK_ROWS = 8
LATE = 2

ANY = pl.BlockSpec(memory_space=pl.ANY)
HBM = pl.BlockSpec(memory_space=pltpu.HBM)
VMEM = pl.BlockSpec(memory_space=pltpu.VMEM)
SMEM = pl.BlockSpec(memory_space=pltpu.SMEM)


def pairs_of(k, n):
    assert n & (n - 1) == 0, n
    return [(i, i ^ k) for i in range(n)]


def call(body, out_shape, in_specs, out_specs, args, scratch=(), limit=None, flops=0):
    size = sum(a.size * a.dtype.itemsize for a in args)
    return pl.pallas_call(
        body,
        out_shape=out_shape,
        in_specs=in_specs,
        out_specs=out_specs,
        scratch_shapes=scratch,
        compiler_params=pltpu.CompilerParams(vmem_limit_bytes=limit),
        cost_estimate=pl.CostEstimate(flops=flops, bytes_accessed=size, transcendentals=0),
    )(*args)


def far(x):
    return pltpu.with_memory_space_constraint(x, pltpu.HBM)


def sequence(n):
    top = [k for k in range(1, n) if 2 * k >= n]
    low = [k for k in range(1, n) if 2 * k < n]
    mixed = top[:1]
    for i in range(len(low)):
        mixed += [top[i + 1], low[i]]
    return [("part", k) for k in mixed] + [("cot", k) for k in mixed]


def split_body(count, rows, wide_ref, *refs):
    outs, sems = refs[:count], refs[count]
    me = lax.axis_index("col")
    copies = []
    for k in range(count):
        start = pl.multiple_of((me ^ k) * rows, rows)
        copies.append(pltpu.make_async_copy(wide_ref.at[:, pl.ds(start, rows)], outs[k], sems.at[k]))
        copies[k].start()
    for copy in copies:
        copy.wait()


def count_body(cols, wide_ref, rows_hbm, lens_hbm, dest_hbm, tile_hbm, counts_ref, plan_ref, *refs):
    outs = refs[:cols]
    rows_ref, lens_ref, slab_ref, dest_ref, tile_ref, sems = refs[cols:]
    pairs, looks, bags = rows_ref.shape
    width = counts_ref.shape[0]
    me = lax.axis_index("col")
    rows_copy = pltpu.make_async_copy(rows_hbm, rows_ref, sems.at[cols])
    lens_copy = pltpu.make_async_copy(lens_hbm, lens_ref, sems.at[cols + 1])
    dest_copy = pltpu.make_async_copy(dest_hbm, dest_ref, sems.at[cols + 2])
    tile_copy = pltpu.make_async_copy(tile_hbm, tile_ref, sems.at[cols + 3])
    for copy in (rows_copy, lens_copy, dest_copy, tile_copy):
        copy.start()
    copies = []
    for k in range(cols):
        start = pl.multiple_of((me ^ k) * width, width)
        copies.append(
            pltpu.make_async_copy(wide_ref.at[:, pl.ds(start, width)], slab_ref.at[k], sems.at[k])
        )
        copies[k].start()
    rows_copy.wait()
    lens_copy.wait()

    def one(p, carry):
        line = lax.broadcasted_iota(jnp.int32, (width, bags), 0)
        lens = lens_ref[pl.ds(p, 1), :]
        total = jnp.zeros((width, bags), jnp.float32)
        for look in range(looks):
            row = rows_ref[p, pl.ds(look, 1), :]
            row = jnp.where(lens > look, row, -1)
            total = total + (line == row).astype(jnp.float32)
        counts_ref[:, pl.ds(pl.multiple_of(p * bags, bags), bags)] = total.astype(jnp.bfloat16)
        return carry

    lax.fori_loop(0, pairs, one, 0)
    dest_copy.wait()
    tile_copy.wait()
    plan_ref[0:1, :] = dest_ref[...]
    plan_ref[1:2, :] = tile_ref[...]
    for k in range(cols):
        copies[k].wait()
        outs[k][...] = slab_ref[k].astype(jnp.bfloat16)


def pool_pairs(span, slabs, counts_ref, wide_ref, put):
    here = lax.axis_index("col")
    thin = slabs[0].shape[0]
    bags = counts_ref.shape[1] // span[1]
    for k, slab_ref in enumerate(slabs):
        first = pl.multiple_of(((here ^ k) % len(slabs)) * thin, thin)
        wide_ref[pl.ds(first, thin), :] = slab_ref[...]
    wide = wide_ref[...]

    def group(g, carry):
        first = pl.multiple_of(g * span[0] * bags, span[0] * bags)
        part = jnp.dot(
            wide, counts_ref[:, pl.ds(first, span[0] * bags)], preferred_element_type=jnp.float32
        )
        for s in range(span[0]):
            put(g * span[0] + s, part[:, s * bags : (s + 1) * bags].T.astype(jnp.bfloat16))
        return carry

    lax.fori_loop(0, span[1] // span[0], group, 0)


def early_body(span, counts_ref, *refs):
    slabs, parts_ref, wide_ref = refs[:-2], refs[-2], refs[-1]

    def put(p, part):
        parts_ref[p] = part

    pool_pairs(span, slabs, counts_ref, wide_ref, put)


def pool_body(tables, cols, span, plan_ref, counts_ref, early_ref, *refs):
    slabs, refs = refs[: cols // 2], refs[cols // 2 :]
    wide_ref, parts_ref, pair_ref = refs[-3:]
    outs = refs[:-3]
    pairs, bags, half = parts_ref.shape
    me = lax.axis_index("table")
    for p in range(pairs):
        pair_ref[plan_ref[0, p] ^ me] = p

    def put(p, part):
        parts_ref[p] = part

    pool_pairs(span, slabs, counts_ref, wide_ref, put)
    side = lax.axis_index("col") // (cols // 2)
    mine = pl.ds(pl.multiple_of(side * bags, bags), bags)
    other = pl.ds(pl.multiple_of((1 - side) * bags, bags), bags)
    lane = lax.broadcasted_iota(jnp.int32, (MARK_ROWS, half), 1)
    for k in range(tables):
        p = pair_ref[k]
        out_ref = outs[k]
        out_ref[mine, :] = early_ref[p]
        out_ref[other, :] = parts_ref[p]
        if k:
            tile = plan_ref[1, p]
            mark = jnp.where(lane < half // 2, tile % 128, tile // 128)
            out_ref[pl.ds(2 * bags, MARK_ROWS), :] = mark.astype(jnp.float32).astype(jnp.bfloat16)


def read_mark(message_ref, bags):
    mark = message_ref[2 * bags :, :].astype(jnp.float32)
    low = lax.broadcasted_iota(jnp.int32, mark.shape, 1) < mark.shape[1] // 2
    units = jnp.max(jnp.where(low, mark, 0.0)).astype(jnp.int32)
    return jnp.max(jnp.where(low, 0.0, mark)).astype(jnp.int32) * 128 + units


def pick_body(bags, grad_ref, message_ref, out_ref):
    tile = read_mark(message_ref, bags)
    out_ref[...] = grad_ref[pl.ds(pl.multiple_of(tile * bags, bags), bags), :]


def own_tile(plan_ref):
    tile, me = 0, lax.axis_index("table")
    for p in range(plan_ref.shape[1]):
        tile = jnp.where(plan_ref[0, p] == me, plan_ref[1, p], tile)
    return tile


def sum_body(plan_ref, own_ref, messages, out_ref, total_ref):
    bags, half = own_ref.shape[0] // 2, own_ref.shape[1]
    tiles = [own_tile(plan_ref)] + [read_mark(message, bags) for message in messages]
    spots = [pl.ds(pl.multiple_of(tile * bags, bags), bags) for tile in tiles]
    out_ref[...] = jnp.zeros_like(out_ref)
    for spot in spots:
        total_ref[spot, :] = jnp.zeros((bags, 2 * half), jnp.float32)
    for spot, block_ref in zip(spots, (own_ref, *messages), strict=True):
        total_ref[spot, :half] += block_ref[:bags, :].astype(jnp.float32)
        total_ref[spot, half:] += block_ref[bags : 2 * bags, :].astype(jnp.float32)
    for spot in spots:
        out_ref[spot, :] = total_ref[spot, :].astype(jnp.bfloat16)


def turn_body(slabs, states, rows_ref, state_ref, wide_ref):
    cols = len(slabs)
    thin = slabs[0].shape[0]
    here = lax.axis_index("col")
    for source, out_ref in ((slabs, rows_ref), (states, state_ref)):
        for k in range(cols):
            first = pl.multiple_of((here ^ k) * thin, thin)
            wide_ref[pl.ds(first, thin), :] = source[k][...].astype(jnp.float32)
        out_ref[...] = wide_ref[...].T.astype(out_ref.dtype)


def ready_body(ahead, late, chunk, plan_ref, grad_ref, counts_ref, messages, sum_ref, counts_late_ref, cots_ref, pair_ref):
    bags = counts_late_ref.shape[1] // len(late)
    me = lax.axis_index("table")
    for p in range(plan_ref.shape[1]):
        pair_ref[plan_ref[0, p] ^ me] = p

    def spot(k):
        return pl.ds(pl.multiple_of(pair_ref[k] * bags, bags), bags)

    for i, k in enumerate(late):
        counts_late_ref[:, i * bags : (i + 1) * bags] = counts_ref[:, spot(k)]
        cots_ref[spot(k), :] = jnp.zeros((bags, cots_ref.shape[1]), cots_ref.dtype)
    tile = own_tile(plan_ref)
    cots_ref[spot(0), :] = grad_ref[pl.ds(pl.multiple_of(tile * bags, bags), bags), :]
    for k, message in zip(ahead, messages, strict=True):
        cots_ref[spot(k), :] = message[...]

    def one(r, carry):
        where = pl.ds(pl.multiple_of(r * chunk, chunk), chunk)
        sum_ref[where, :] = jnp.dot(
            counts_ref[where, :], cots_ref[...], preferred_element_type=jnp.float32
        )
        return carry

    lax.fori_loop(0, counts_ref.shape[0] // chunk, one, 0)


def finish_body(ahead, late, chunk, cols, plan_ref, own_ref, grad_ref, counts_ref, *refs):
    parts = len(ahead) + len(late)
    messages, refs = refs[:parts], refs[parts:]
    cots, refs = refs[: len(ahead)], refs[len(ahead) :]
    slabs, states, refs = refs[:cols], refs[cols : 2 * cols], refs[2 * cols :]
    pooled_out, rows_ref, state_ref, sum_ref, late_ref = refs[:5]
    pooled_ref, total_ref, wide_ref, cots_ref, pair_ref, sem = refs[5:]
    sum_body(plan_ref, own_ref, messages, pooled_ref, total_ref)
    copy = pltpu.make_async_copy(pooled_ref, pooled_out, sem)
    copy.start()
    ready_body(ahead, late, chunk, plan_ref, grad_ref, counts_ref, cots, sum_ref, late_ref, cots_ref, pair_ref)
    turn_body(slabs, states, rows_ref, state_ref, wide_ref)
    copy.wait()


def update_body(chunk, sum_ref, counts_ref, rows_ref, state_ref, *refs):
    messages = refs[:-6]
    out_rows_ref, out_state_ref, new_rows_ref, new_state_ref, cots_ref, sems = refs[-6:]
    bags = counts_ref.shape[1] // len(messages)
    for i, message in enumerate(messages):
        cots_ref[i * bags : (i + 1) * bags, :] = message[...]
    copies = []
    for r in range(counts_ref.shape[0] // chunk):
        where = pl.ds(r * chunk, chunk)
        grad = sum_ref[where, :] + jnp.dot(
            counts_ref[where, :], cots_ref[...], preferred_element_type=jnp.float32
        )
        state = state_ref[where, :].astype(jnp.float32) + grad * grad
        rows = rows_ref[where, :].astype(jnp.float32)
        new_state_ref[where, :] = state
        new_rows_ref[where, :] = (
            rows - LEARN_RATE * grad / (jnp.sqrt(state) + EPSILON)
        ).astype(jnp.bfloat16)
        for i, (src, dst) in enumerate(((new_state_ref, out_state_ref), (new_rows_ref, out_rows_ref))):
            copy = pltpu.make_async_copy(src.at[where], dst.at[where], sems.at[r, i])
            copy.start()
            copies.append(copy)
    for copy in copies:
        copy.wait()


def per_device(embedding, accumulator, pair_rows, pair_len, pair_dest, pair_tile, pooled_grad):
    tables, cols = lax.axis_size("table"), lax.axis_size("col")
    pairs, bags, looks = pair_rows.shape
    thin = embedding.shape[1]
    width = thin * cols
    rows = embedding.shape[0] // cols
    span = min(8, pairs)
    chunk = min(256, rows)
    shape, near = jax.ShapeDtypeStruct, pltpu.VMEM
    bf16 = jnp.bfloat16
    mega = 1 << 20
    spare = pairs * bags * width * 2
    big = 12 * mega + 3 * spare

    def over_col(parts):
        moved = {k: lax.ppermute(parts[k], "col", pairs_of(k, cols)) for k in range(1, cols)}
        return [parts[0]] + [moved[k] for k in range(1, cols)]

    slabs = call(
        functools.partial(split_body, cols, rows),
        [near((thin, rows), bf16)] * cols,
        [HBM],
        [VMEM] * cols,
        (far(embedding.T),),
        scratch=[pltpu.SemaphoreType.DMA((cols,))],
        limit=8 * mega,
    )
    slabs = over_col(slabs)
    counts, plan, *states = call(
        functools.partial(count_body, cols),
        [near((rows, pairs * bags), bf16), near((2, pairs), jnp.int32)] + [near((thin, rows), bf16)] * cols,
        [HBM] * 5,
        [VMEM] * (2 + cols),
        (
            far(accumulator.T),
            far(jnp.transpose(pair_rows, (0, 2, 1))),
            far(pair_len),
            far(pair_dest),
            far(pair_tile),
        ),
        scratch=[
            pltpu.VMEM((pairs, looks, bags), jnp.int32),
            pltpu.VMEM((pairs, bags), jnp.int32),
            pltpu.VMEM((cols, thin, rows), jnp.float32),
            pltpu.VMEM((1, pairs), jnp.int32),
            pltpu.VMEM((1, pairs), jnp.int32),
            pltpu.SemaphoreType.DMA((cols + 4,)),
        ],
        limit=8 * mega,
    )
    states = over_col(states)

    half, count = width // 2, (span, pairs)
    early = call(
        functools.partial(early_body, count),
        near((pairs, bags, half), bf16),
        [VMEM] * (1 + cols // 2),
        VMEM,
        (counts, *slabs[: cols // 2]),
        scratch=[pltpu.VMEM((half, rows), bf16)],
        limit=big,
        flops=rows * width * pairs * bags,
    )
    own_block, *blocks = call(
        functools.partial(pool_body, tables, cols, count),
        [near((2 * bags + (MARK_ROWS if k else 0), half), bf16) for k in range(tables)],
        [SMEM, VMEM, VMEM] + [VMEM] * (cols // 2),
        [VMEM] * tables,
        (plan, counts, early, *slabs[cols // 2 :]),
        scratch=[
            pltpu.VMEM((half, rows), bf16),
            pltpu.VMEM((pairs, bags, half), bf16),
            pltpu.SMEM((pairs,), jnp.int32),
        ],
        limit=big,
        flops=rows * width * pairs * bags,
    )
    arrived, returned = {}, {}
    for kind, k in sequence(tables):
        if kind == "part":
            arrived[k] = lax.ppermute(blocks[k - 1], "table", pairs_of(k, tables))
        else:
            picked = call(
                functools.partial(pick_body, bags),
                near((bags, width), bf16),
                [VMEM, VMEM],
                VMEM,
                (pooled_grad, arrived[k]),
                limit=8 * mega,
            )
            returned[k] = lax.ppermute(picked, "table", pairs_of(k, tables))

    cut = max(len(returned) - LATE, 0)
    ahead, late = list(returned)[:cut], list(returned)[cut:]
    pooled, *turned, so_far, counts_late = call(
        functools.partial(
            finish_body, ahead, late, min(512, rows), cols
        ),
        [shape(pooled_grad.shape, bf16)]
        + [near((rows, width), bf16)] * 2
        + [near((rows, width), jnp.float32), near((rows, len(late) * bags), bf16)],
        [SMEM] + [VMEM] * (3 + len(arrived) + len(ahead) + 2 * cols),
        [ANY] + [VMEM] * 4,
        (
            plan,
            own_block,
            pooled_grad,
            counts,
            *arrived.values(),
            *[returned[k] for k in ahead],
            *slabs,
            *states,
        ),
        scratch=[
            pltpu.VMEM(pooled_grad.shape, bf16),
            pltpu.VMEM(pooled_grad.shape, jnp.float32),
            pltpu.VMEM((width, rows), jnp.float32),
            pltpu.VMEM((pairs * bags, width), bf16),
            pltpu.SMEM((pairs,), jnp.int32),
            pltpu.SemaphoreType.DMA,
        ],
        limit=big,
        flops=2 * rows * width * pairs * bags,
    )
    new_rows, new_state = call(
        functools.partial(update_body, chunk),
        [shape((rows, width), bf16), shape((rows, width), jnp.float32)],
        [VMEM] * (4 + len(late)),
        [ANY, ANY],
        (so_far, counts_late, *turned, *[returned[k] for k in late]),
        scratch=[
            pltpu.VMEM((rows, width), bf16),
            pltpu.VMEM((rows, width), jnp.float32),
            pltpu.VMEM((len(late) * bags, width), bf16),
            pltpu.SemaphoreType.DMA((rows // chunk, 2)),
        ],
        limit=big,
        flops=2 * rows * width * len(late) * bags,
    )
    return (pooled, new_rows, new_state)


def solution(mesh):
    return jax.shard_map(
        per_device,
        mesh=mesh,
        in_specs=(
            P("table", "col"),
            P("table", "col"),
            P(("table", "col"), None, None),
            P(("table", "col"), None),
            P(("table", "col"), None),
            P(("table", "col"), None),
            P(("table", "col"), None),
        ),
        out_specs=(P(("table", "col"), None), P(("table", "col"), None), P(("table", "col"), None)),
        check_vma=False,
    )
```

time: 51.7 us -> 47.9 us (0.926)
  waiting for transfers between devices: 10.6 us -> 9.24 us
  Pallas kernels: 11.3 us -> 10.4 us
  other arithmetic: 0.68 us -> 0 us
    ppermute x6, waiting for transfers between devices: 3.28 us -> 1.3 us  [over_col(): lax.ppermute(parts[k], 'col', pairs_of(k, cols))]
    ppermute x14, starting transfers between devices: 22.6 us -> 20.8 us  [the longest x7 11.6 us: per_device(): arrived[k] = lax.ppermute(blocks[k - 1], 'table', pairs_of(k, tables))]
    ppermute x6, starting transfers between devices: 5.11 us -> 6.41 us  [over_col(): lax.ppermute(parts[k], 'col', pairs_of(k, cols))]
    pallas_call x13, Pallas kernels: 11.3 us -> 10.4 us  [call(): pl.pallas_call(body, out_shape=out_shape, in_specs=in_specs, out_specs=ou...]
    concatenate x1 -> x0, other arithmetic: 0.68 us -> none  [per_device(): plan = jnp.concatenate([pair_dest, pair_tile])]
    ppermute x14, waiting for transfers between devices: 7.31 us -> 7.94 us  [the longest x7 6.04 us: per_device(): returned[k] = lax.ppermute(picked, 'table', pairs_of(k, tables))]
  transfers between devices with their start and end apart: 20 -> 20, of which waited for: 4 -> 6; matrix products, arithmetic and copies ran while one was open for 1% -> 0% of each run, Pallas kernels for 12% -> 16%
where the time goes in v1:
time: 47.9 us; the launch traced here: 47.6 us
  starting transfers between devices  27.2 us (57%)
  Pallas kernels  10.4 us (22%)
  waiting for transfers between devices  9.24 us (19%)
  between operations  0.77 us (2%)
    ppermute x7, starting transfers between devices, per_device(): arrived[k] = lax.ppermute(blocks[k - 1], 'table', pairs_of(k, tables))  11.6 us
    pallas_call x13, Pallas kernels, call(): pl.pallas_call(body, out_shape=out_shape, in_specs=in_specs, out_specs=ou...  10.4 us
    ppermute x7, starting transfers between devices, per_device(): returned[k] = lax.ppermute(picked, 'table', pairs_of(k, tables))  9.22 us
    ppermute x6, starting transfers between devices, over_col(): lax.ppermute(parts[k], 'col', pairs_of(k, cols))  6.41 us
    ppermute x7, waiting for transfers between devices, per_device(): returned[k] = lax.ppermute(picked, 'table', pairs_of(k, tables))  6.04 us
    ppermute x7, waiting for transfers between devices, per_device(): arrived[k] = lax.ppermute(blocks[k - 1], 'table', pairs_of(k, tables))  1.9 us
    ppermute x6, waiting for transfers between devices, over_col(): lax.ppermute(parts[k], 'col', pairs_of(k, cols))  1.3 us
  transfers between devices with their start and end apart: 20, of which 6 were waited for; matrix products, arithmetic and copies ran while one was open for 0% of the time, Pallas kernels for 16%

profile of v1, /device:TPU:0, one launch (start us, length us, event | category | flops | bytes accessed | tf_op | source)
XLA Modules:
  0.0 47.6 jit_solution(471385556039008770)
XLA Ops:
  0.6 1.1 %shard_map.95 = (bf16[64,1024]{1,0:T(8,128)(2,1)S(1)}, bf16[64,1024]{1,0:T(8,128)(2,1)S(1)}, bf16[64,1024]{1,0:T(8,128)(2,1)S(1)}, bf16[64,1024]{1,0:T(8,128)(2,1)S(1)}) custom-call(bf16[64,4096]{1,0:T(8,128)(2,1)} %bitcast.4), custom_call_target="tpu_custom_call" | custom-call | bytes 524288 | tf_op jit(solution)/shard_map/pallas_call | solution.py:29
  1.8 0.6 %collective-permute-start = (bf16[64,1024]{1,0:T(8,128)(2,1)S(1)}, bf16[64,1024]{1,0:T(8,128)(2,1)S(1)}, u32[]{:S(2)}, u32[]{:S(2)}) collective-permute-start(bf16[64,1024]{1,0:T(8,128)(2,1)S(1)} %get-tuple-element.31), channel_id=1, source_target_pairs={{0,1},{1,0},{2,3},{3,2},{4,5},{5,4},{6,7},{7,6},{8,9},{9,8},{10,11... | collective-permute-start | bytes 393224 | tf_op jit(solution)/shard_map/ppermute | solution.py:293
  2.3 2.6 %collective-permute-start.1 = (bf16[64,1024]{1,0:T(8,128)(2,1)S(1)}, bf16[64,1024]{1,0:T(8,128)(2,1)S(1)}, u32[]{:S(2)}, u32[]{:S(2)}) collective-permute-start(bf16[64,1024]{1,0:T(8,128)(2,1)S(1)} %get-tuple-element.32), channel_id=1, source_target_pairs={{0,2},{1,3},{2,0},{3,1},{4,6},{5,7},{6,4},{7,5},{8,10},{9,11},{10,... | collective-permute-start | bytes 393224 | tf_op jit(solution)/shard_map/ppermute | solution.py:293
  4.9 2.7 %shard_map.94 = (bf16[1024,1024]{1,0:T(8,128)(2,1)S(1)}, s32[2,8]{1,0:T(2,128)S(1)}, bf16[64,1024]{1,0:T(8,128)(2,1)S(1)}, bf16[64,1024]{1,0:T(8,128)(2,1)S(1)},...) custom-call(f32[64,4096]{1,0:T(8,128)} %bitcast.3, s32[8,4,128]{2,1,0:T(4,128)} %bitcast.5, ...), custom_call_target="tpu_custom_call" | custom-call | bytes 1069120 | tf_op jit(solution)/shard_map/pallas_call | solution.py:29
  7.6 0.2 collective-permute-start.15
  7.8 1.9 %collective-permute-start.16 = (bf16[64,1024]{1,0:T(8,128)(2,1)S(1)}, bf16[64,1024]{1,0:T(8,128)(2,1)S(1)}, u32[]{:S(2)}, u32[]{:S(2)}) collective-permute-start(bf16[64,1024]{1,0:T(8,128)(2,1)S(1)} %get-tuple-element.44), channel_id=1, source_target_pairs={{0,2},{1,3},{2,0},{3,1},{4,6},{5,7},{6,4},{7,5},{8,10},{9,11},{10,... | collective-permute-start | bytes 393224 | tf_op jit(solution)/shard_map/ppermute | solution.py:293
  9.8 0.5 %shard_map.96.early_ref = bf16[8,128,128]{2,1,0:T(8,128)(2,1)S(1)} custom-call(bf16[1024,1024]{1,0:T(8,128)(2,1)S(1)} %get-tuple-element.29.counts_ref, bf16[64,1024]{1,0:T(8,128)(2,1)S(1)} %get-tuple-element.30.refs_0_.refs_12_, bf16[64,1024]{1,0:T(8,128)(2,1)S(1)} %collective-permute-done.refs_1_.refs_13_), custom_call_target="tpu_custom_call" | custom-call | flops 268435456 | bytes 2359296 | tf_op jit(solution)/shard_map/pallas_call | solution.py:29
  10.3 1.3 %collective-permute-done.2.refs_1_.refs_15_ = bf16[64,1024]{1,0:T(8,128)(2,1)S(1)} collective-permute-done((bf16[64,1024]{1,0:T(8,128)(2,1)S(1)}, bf16[64,1024]{1,0:T(8,128)(2,1)S(1)}, u32[]{:S(2)}, u32[]{:S(2)}) %collective-permute-start.2) | collective-permute-done | bytes 131104 | tf_op jit(solution)/shard_map/ppermute | solution.py:293
  11.6 1.1 %shard_map.97 = (bf16[256,128]{1,0:T(8,128)(2,1)S(1)}, bf16[264,128]{1,0:T(8,128)(2,1)S(1)}, bf16[264,128]{1,0:T(8,128)(2,1)S(1)}, bf16[264,128]{1,0:T(8,128)(2,...) custom-call(s32[2,8]{1,0:T(2,128)S(1)} %get-tuple-element.28.plan_re, ...), custom_call_target="tpu_custom_call" | custom-call | flops 268435456 | bytes 2621504 | tf_op jit(solution)/shard_map/pallas_call | solution.py:29
  12.7 2.7 %collective-permute-start.3 = (bf16[264,128]{1,0:T(8,128)(2,1)S(1)}, bf16[264,128]{1,0:T(8,128)(2,1)S(1)}, u32[]{:S(2)}, u32[]{:S(2)}) collective-permute-start(bf16[264,128]{1,0:T(8,128)(2,1)S(1)} %get-tuple-element.35), channel_id=1, source_target_pairs={{0,16},{4,20},{8,24},{12,28},{16,0},{20,4},{24,8},{28,12},{1,17},{... | collective-permute-start | bytes 202760 | tf_op jit(solution)/shard_map/ppermute | solution.py:358
  15.4 1.3 %collective-permute-start.4 = (bf16[264,128]{1,0:T(8,128)(2,1)S(1)}, bf16[264,128]{1,0:T(8,128)(2,1)S(1)}, u32[]{:S(2)}, u32[]{:S(2)}) collective-permute-start(bf16[264,128]{1,0:T(8,128)(2,1)S(1)} %get-tuple-element.36), channel_id=1, source_target_pairs={{0,20},{4,16},{8,28},{12,24},{16,4},{20,0},{24,12},{28,8},{1,21},{... | collective-permute-start | bytes 202760 | tf_op jit(solution)/shard_map/ppermute | solution.py:358
  16.6 0.5 %collective-permute-start.5 = (bf16[264,128]{1,0:T(8,128)(2,1)S(1)}, bf16[264,128]{1,0:T(8,128)(2,1)S(1)}, u32[]{:S(2)}, u32[]{:S(2)}) collective-permute-start(bf16[264,128]{1,0:T(8,128)(2,1)S(1)} %get-tuple-element.37), channel_id=1, source_target_pairs={{0,4},{4,0},{8,12},{12,8},{16,20},{20,16},{24,28},{28,24},{1,5},{5... | collective-permute-start | bytes 202760 | tf_op jit(solution)/shard_map/ppermute | solution.py:358
  17.2 1.1 %collective-permute-start.17 = (bf16[64,1024]{1,0:T(8,128)(2,1)S(1)}, bf16[64,1024]{1,0:T(8,128)(2,1)S(1)}, u32[]{:S(2)}, u32[]{:S(2)}) collective-permute-start(bf16[64,1024]{1,0:T(8,128)(2,1)S(1)} %get-tuple-element.45), channel_id=1, source_target_pairs={{0,3},{1,2},{2,1},{3,0},{4,7},{5,6},{6,5},{7,4},{8,11},{9,10},{10,... | collective-permute-start | bytes 393224 | tf_op jit(solution)/shard_map/ppermute | solution.py:293
  18.2 3.6 %collective-permute-start.6 = (bf16[264,128]{1,0:T(8,128)(2,1)S(1)}, bf16[264,128]{1,0:T(8,128)(2,1)S(1)}, u32[]{:S(2)}, u32[]{:S(2)}) collective-permute-start(bf16[264,128]{1,0:T(8,128)(2,1)S(1)} %get-tuple-element.38), channel_id=1, source_target_pairs={{0,24},{4,28},{8,16},{12,20},{16,8},{20,12},{24,0},{28,4},{1,25},{... | collective-permute-start | bytes 202760 | tf_op jit(solution)/shard_map/ppermute | solution.py:358
  21.8 0.3 collective-permute-start.7
  22.1 1.9 %collective-permute-done.4.message_ref.refs_1_ = bf16[264,128]{1,0:T(8,128)(2,1)S(1)} collective-permute-done((bf16[264,128]{1,0:T(8,128)(2,1)S(1)}, bf16[264,128]{1,0:T(8,128)(2,1)S(1)}, u32[]{:S(2)}, u32[]{:S(2)}) %collective-permute-start.4) | collective-permute-done | bytes 67616 | tf_op jit(solution)/shard_map/ppermute | solution.py:358
  24.0 3.3 %collective-permute-start.8 = (bf16[264,128]{1,0:T(8,128)(2,1)S(1)}, bf16[264,128]{1,0:T(8,128)(2,1)S(1)}, u32[]{:S(2)}, u32[]{:S(2)}) collective-permute-start(bf16[264,128]{1,0:T(8,128)(2,1)S(1)} %get-tuple-element.40), channel_id=1, source_target_pairs={{0,28},{4,24},{8,20},{12,16},{16,12},{20,8},{24,4},{28,0},{1,29},{... | collective-permute-start | bytes 202760 | tf_op jit(solution)/shard_map/ppermute | solution.py:358
  27.3 0.1 shard_map.98
  27.4 0.1 shard_map.99
  27.6 2.1 %collective-permute-start.10 = (bf16[128,256]{1,0:T(8,128)(2,1)S(1)}, bf16[128,256]{1,0:T(8,128)(2,1)S(1)}, u32[]{:S(2)}, u32[]{:S(2)}) collective-permute-start(bf16[128,256]{1,0:T(8,128)(2,1)S(1)} %shard_map.98), channel_id=1, source_target_pairs={{0,16},{4,20},{8,24},{12,28},{16,0},{20,4},{24,8},{28,12},{1,17},{... | collective-permute-start | bytes 196616 | tf_op jit(solution)/shard_map/ppermute | solution.py:368
  29.6 2.0 %collective-permute-start.11 = (bf16[128,256]{1,0:T(8,128)(2,1)S(1)}, bf16[128,256]{1,0:T(8,128)(2,1)S(1)}, u32[]{:S(2)}, u32[]{:S(2)}) collective-permute-start(bf16[128,256]{1,0:T(8,128)(2,1)S(1)} %shard_map.99), channel_id=1, source_target_pairs={{0,20},{4,16},{8,28},{12,24},{16,4},{20,0},{24,12},{28,8},{1,21},{... | collective-permute-start | bytes 196616 | tf_op jit(solution)/shard_map/ppermute | solution.py:368
  31.9 0.1 shard_map.102
  32.1 0.5 %collective-permute-start.12 = (bf16[128,256]{1,0:T(8,128)(2,1)S(1)}, bf16[128,256]{1,0:T(8,128)(2,1)S(1)}, u32[]{:S(2)}, u32[]{:S(2)}) collective-permute-start(bf16[128,256]{1,0:T(8,128)(2,1)S(1)} %shard_map.100), channel_id=1, source_target_pairs={{0,4},{4,0},{8,12},{12,8},{16,20},{20,16},{24,28},{28,24},{1,5},{5... | collective-permute-start | bytes 196616 | tf_op jit(solution)/shard_map/ppermute | solution.py:368
  32.6 2.4 %collective-permute-start.13 = (bf16[128,256]{1,0:T(8,128)(2,1)S(1)}, bf16[128,256]{1,0:T(8,128)(2,1)S(1)}, u32[]{:S(2)}, u32[]{:S(2)}) collective-permute-start(bf16[128,256]{1,0:T(8,128)(2,1)S(1)} %shard_map.101), channel_id=1, source_target_pairs={{0,24},{4,28},{8,16},{12,20},{16,8},{20,12},{24,0},{28,4},{1,25},{... | collective-permute-start | bytes 196616 | tf_op jit(solution)/shard_map/ppermute | solution.py:368
  35.0 0.6 %collective-permute-start.14 = (bf16[128,256]{1,0:T(8,128)(2,1)S(1)}, bf16[128,256]{1,0:T(8,128)(2,1)S(1)}, u32[]{:S(2)}, u32[]{:S(2)}) collective-permute-start(bf16[128,256]{1,0:T(8,128)(2,1)S(1)} %shard_map.102), channel_id=1, source_target_pairs={{0,8},{4,12},{8,0},{12,4},{16,24},{20,28},{24,16},{28,20},{1,9},{5... | collective-permute-start | bytes 196616 | tf_op jit(solution)/shard_map/ppermute | solution.py:368
  35.9 1.2 %collective-permute-done.10.refs_7_ = bf16[128,256]{1,0:T(8,128)(2,1)S(1)} collective-permute-done((bf16[128,256]{1,0:T(8,128)(2,1)S(1)}, bf16[128,256]{1,0:T(8,128)(2,1)S(1)}, u32[]{:S(2)}, u32[]{:S(2)}) %collective-permute-start.10) | collective-permute-done | bytes 65568 | tf_op jit(solution)/shard_map/ppermute | solution.py:368
  37.1 1.6 %collective-permute-start.18 = (bf16[128,256]{1,0:T(8,128)(2,1)S(1)}, bf16[128,256]{1,0:T(8,128)(2,1)S(1)}, u32[]{:S(2)}, u32[]{:S(2)}) collective-permute-start(bf16[128,256]{1,0:T(8,128)(2,1)S(1)} %shard_map.104), channel_id=1, source_target_pairs={{0,28},{4,24},{8,20},{12,16},{16,12},{20,8},{24,4},{28,0},{1,29},{... | collective-permute-start | bytes 196616 | tf_op jit(solution)/shard_map/ppermute | solution.py:368
  38.7 2.1 %collective-permute-done.11.refs_8_ = bf16[128,256]{1,0:T(8,128)(2,1)S(1)} collective-permute-done((bf16[128,256]{1,0:T(8,128)(2,1)S(1)}, bf16[128,256]{1,0:T(8,128)(2,1)S(1)}, u32[]{:S(2)}, u32[]{:S(2)}) %collective-permute-start.11) | collective-permute-done | bytes 65568 | tf_op jit(solution)/shard_map/ppermute | solution.py:368
  40.8 2.4 %shard_map.103 = (bf16[2048,256]{1,0:T(8,128)(2,1)}, bf16[1024,256]{1,0:T(8,128)(2,1)S(1)}, bf16[1024,256]{1,0:T(8,128)(2,1)S(1)}, f32[1024,256]{1,0:T(8,128)S(1)}, bf16[1024,256]{1,0:T(8,128)(2,1)S(1)}) custom-call(s32[2,8]{1,0:T(2,128)S(1)} %get-tuple-element.28.plan_ref, bf16[256,128]{1,0:T(8,128)(2,1)S(1)} %get-tuple-element.34.own_ref, ...), custom_call_target="tpu_custom_call" | custom-call | flops 536870912 | bytes 5060672 | tf_op jit(solution)/shard_map/pallas_call | solution.py:29
  43.2 0.9 %collective-permute-done.18.refs_0_ = bf16[128,256]{1,0:T(8,128)(2,1)S(1)} collective-permute-done((bf16[128,256]{1,0:T(8,128)(2,1)S(1)}, bf16[128,256]{1,0:T(8,128)(2,1)S(1)}, u32[]{:S(2)}, u32[]{:S(2)}) %collective-permute-start.18) | collective-permute-done | bytes 65568 | tf_op jit(solution)/shard_map/ppermute | solution.py:368
  44.1 1.8 %collective-permute-done.19.refs_1_ = bf16[128,256]{1,0:T(8,128)(2,1)S(1)} collective-permute-done((bf16[128,256]{1,0:T(8,128)(2,1)S(1)}, bf16[128,256]{1,0:T(8,128)(2,1)S(1)}, u32[]{:S(2)}, u32[]{:S(2)}) %collective-permute-start.19) | collective-permute-done | bytes 65568 | tf_op jit(solution)/shard_map/ppermute | solution.py:368
  45.9 1.7 %shard_map.106 = (bf16[1024,256]{1,0:T(8,128)(2,1)}, f32[1024,256]{1,0:T(8,128)}) custom-call(f32[1024,256]{1,0:T(8,128)S(1)} %get-tuple-element.47.sum_ref, bf16[1024,256]{1,0:T(8,128)(2,1)S(1)} %get-tuple-element.48.counts_ref, bf16[1024,256]{1,0:T(8,128)(2,1)S(1)} %get-tuple-element.49.rows_ref, bf16[1024,256]{1,0:T(8,128)(2,1)S(1)} %get-tuple-element.50.state_ref, ...), custom_call_target="tpu_custom_call" | custom-call | flops 134217728 | bytes 2752512 | tf_op jit(solution)/shard_map/pallas_call | solution.py:29
  (23 shorter events, 0.6 us)
Async XLA Ops:
  1.8 8.0 %collective-permute-start = (bf16[64,1024]{1,0:T(8,128)(2,1)S(1)}, bf16[64,1024]{1,0:T(8,128)(2,1)S(1)}, u32[]{:S(2)}, u32[]{:S(2)}) collective-permute-start(bf16[64,1024]{1,0:T(8,128)(2,1)S(1)} %get-tuple-element.31), channel_id=1, source_target_pairs={{0,1},{1,0},{2,3},{3,2},{4,5},{5,4},{6,7},{7,6},{8,9},{9,8},{10,11... | collective-permute-start | bytes 393224 | tf_op jit(solution)/shard_map/ppermute | solution.py:293
  2.3 8.0 %collective-permute-start.1 = (bf16[64,1024]{1,0:T(8,128)(2,1)S(1)}, bf16[64,1024]{1,0:T(8,128)(2,1)S(1)}, u32[]{:S(2)}, u32[]{:S(2)}) collective-permute-start(bf16[64,1024]{1,0:T(8,128)(2,1)S(1)} %get-tuple-element.32), channel_id=1, source_target_pairs={{0,2},{1,3},{2,0},{3,1},{4,6},{5,7},{6,4},{7,5},{8,10},{9,11},{10,... | collective-permute-start | bytes 393224 | tf_op jit(solution)/shard_map/ppermute | solution.py:293
  4.9 6.7 %collective-permute-start.2 = (bf16[64,1024]{1,0:T(8,128)(2,1)S(1)}, bf16[64,1024]{1,0:T(8,128)(2,1)S(1)}, u32[]{:S(2)}, u32[]{:S(2)}) collective-permute-start(bf16[64,1024]{1,0:T(8,128)(2,1)S(1)} %get-tuple-element.33), channel_id=1, source_target_pairs={{0,3},{1,2},{2,1},{3,0},{4,7},{5,6},{6,5},{7,4},{8,11},{9,10},{10,... | collective-permute-start | bytes 393224 | tf_op jit(solution)/shard_map/ppermute | solution.py:293
  7.6 9.6 %collective-permute-start.15 = (bf16[64,1024]{1,0:T(8,128)(2,1)S(1)}, bf16[64,1024]{1,0:T(8,128)(2,1)S(1)}, u32[]{:S(2)}, u32[]{:S(2)}) collective-permute-start(bf16[64,1024]{1,0:T(8,128)(2,1)S(1)} %get-tuple-element.43), channel_id=1, source_target_pairs={{0,1},{1,0},{2,3},{3,2},{4,5},{5,4},{6,7},{7,6},{8,9},{9,8},{10,11... | collective-permute-start | bytes 393224 | tf_op jit(solution)/shard_map/ppermute | solution.py:293
  7.8 10.4 %collective-permute-start.16 = (bf16[64,1024]{1,0:T(8,128)(2,1)S(1)}, bf16[64,1024]{1,0:T(8,128)(2,1)S(1)}, u32[]{:S(2)}, u32[]{:S(2)}) collective-permute-start(bf16[64,1024]{1,0:T(8,128)(2,1)S(1)} %get-tuple-element.44), channel_id=1, source_target_pairs={{0,2},{1,3},{2,0},{3,1},{4,6},{5,7},{6,4},{7,5},{8,10},{9,11},{10,... | collective-permute-start | bytes 393224 | tf_op jit(solution)/shard_map/ppermute | solution.py:293
  9.8 17.5 %copy-start = (bf16[2048,256]{1,0:T(8,128)(2,1)S(1)}, bf16[2048,256]{1,0:T(8,128)(2,1)}, u32[]{:S(2)}) copy-start(bf16[2048,256]{1,0:T(8,128)(2,1)} %grad_ref.15) | copy-start | bytes 3145732
  12.7 9.1 %collective-permute-start.3 = (bf16[264,128]{1,0:T(8,128)(2,1)S(1)}, bf16[264,128]{1,0:T(8,128)(2,1)S(1)}, u32[]{:S(2)}, u32[]{:S(2)}) collective-permute-start(bf16[264,128]{1,0:T(8,128)(2,1)S(1)} %get-tuple-element.35), channel_id=1, source_target_pairs={{0,16},{4,20},{8,24},{12,28},{16,0},{20,4},{24,8},{28,12},{1,17},{... | collective-permute-start | bytes 202760 | tf_op jit(solution)/shard_map/ppermute | solution.py:358
  15.4 8.6 %collective-permute-start.4 = (bf16[264,128]{1,0:T(8,128)(2,1)S(1)}, bf16[264,128]{1,0:T(8,128)(2,1)S(1)}, u32[]{:S(2)}, u32[]{:S(2)}) collective-permute-start(bf16[264,128]{1,0:T(8,128)(2,1)S(1)} %get-tuple-element.36), channel_id=1, source_target_pairs={{0,20},{4,16},{8,28},{12,24},{16,4},{20,0},{24,12},{28,8},{1,21},{... | collective-permute-start | bytes 202760 | tf_op jit(solution)/shard_map/ppermute | solution.py:358
  16.6 10.6 %collective-permute-start.5 = (bf16[264,128]{1,0:T(8,128)(2,1)S(1)}, bf16[264,128]{1,0:T(8,128)(2,1)S(1)}, u32[]{:S(2)}, u32[]{:S(2)}) collective-permute-start(bf16[264,128]{1,0:T(8,128)(2,1)S(1)} %get-tuple-element.37), channel_id=1, source_target_pairs={{0,4},{4,0},{8,12},{12,8},{16,20},{20,16},{24,28},{28,24},{1,5},{5... | collective-permute-start | bytes 202760 | tf_op jit(solution)/shard_map/ppermute | solution.py:358
  17.2 14.9 %collective-permute-start.17 = (bf16[64,1024]{1,0:T(8,128)(2,1)S(1)}, bf16[64,1024]{1,0:T(8,128)(2,1)S(1)}, u32[]{:S(2)}, u32[]{:S(2)}) collective-permute-start(bf16[64,1024]{1,0:T(8,128)(2,1)S(1)} %get-tuple-element.45), channel_id=1, source_target_pairs={{0,3},{1,2},{2,1},{3,0},{4,7},{5,6},{6,5},{7,4},{8,11},{9,10},{10,... | collective-permute-start | bytes 393224 | tf_op jit(solution)/shard_map/ppermute | solution.py:293
  18.2 9.3 %collective-permute-start.6 = (bf16[264,128]{1,0:T(8,128)(2,1)S(1)}, bf16[264,128]{1,0:T(8,128)(2,1)S(1)}, u32[]{:S(2)}, u32[]{:S(2)}) collective-permute-start(bf16[264,128]{1,0:T(8,128)(2,1)S(1)} %get-tuple-element.38), channel_id=1, source_target_pairs={{0,24},{4,28},{8,16},{12,20},{16,8},{20,12},{24,0},{28,4},{1,25},{... | collective-permute-start | bytes 202760 | tf_op jit(solution)/shard_map/ppermute | solution.py:358
  21.8 7.8 %collective-permute-start.7 = (bf16[264,128]{1,0:T(8,128)(2,1)S(1)}, bf16[264,128]{1,0:T(8,128)(2,1)S(1)}, u32[]{:S(2)}, u32[]{:S(2)}) collective-permute-start(bf16[264,128]{1,0:T(8,128)(2,1)S(1)} %get-tuple-element.39), channel_id=1, source_target_pairs={{0,8},{4,12},{8,0},{12,4},{16,24},{20,28},{24,16},{28,20},{1,9},{5... | collective-permute-start | bytes 202760 | tf_op jit(solution)/shard_map/ppermute | solution.py:358
  24.0 8.6 %collective-permute-start.8 = (bf16[264,128]{1,0:T(8,128)(2,1)S(1)}, bf16[264,128]{1,0:T(8,128)(2,1)S(1)}, u32[]{:S(2)}, u32[]{:S(2)}) collective-permute-start(bf16[264,128]{1,0:T(8,128)(2,1)S(1)} %get-tuple-element.40), channel_id=1, source_target_pairs={{0,28},{4,24},{8,20},{12,16},{16,12},{20,8},{24,4},{28,0},{1,29},{... | collective-permute-start | bytes 202760 | tf_op jit(solution)/shard_map/ppermute | solution.py:358
  27.3 7.8 %collective-permute-start.9 = (bf16[264,128]{1,0:T(8,128)(2,1)S(1)}, bf16[264,128]{1,0:T(8,128)(2,1)S(1)}, u32[]{:S(2)}, u32[]{:S(2)}) collective-permute-start(bf16[264,128]{1,0:T(8,128)(2,1)S(1)} %get-tuple-element.41), channel_id=1, source_target_pairs={{0,12},{4,8},{8,4},{12,0},{16,28},{20,24},{24,20},{28,16},{1,13},{... | collective-permute-start | bytes 202760 | tf_op jit(solution)/shard_map/ppermute | solution.py:358
  27.6 9.6 %collective-permute-start.10 = (bf16[128,256]{1,0:T(8,128)(2,1)S(1)}, bf16[128,256]{1,0:T(8,128)(2,1)S(1)}, u32[]{:S(2)}, u32[]{:S(2)}) collective-permute-start(bf16[128,256]{1,0:T(8,128)(2,1)S(1)} %shard_map.98), channel_id=1, source_target_pairs={{0,16},{4,20},{8,24},{12,28},{16,0},{20,4},{24,8},{28,12},{1,17},{... | collective-permute-start | bytes 196616 | tf_op jit(solution)/shard_map/ppermute | solution.py:368
  29.6 11.1 %collective-permute-start.11 = (bf16[128,256]{1,0:T(8,128)(2,1)S(1)}, bf16[128,256]{1,0:T(8,128)(2,1)S(1)}, u32[]{:S(2)}, u32[]{:S(2)}) collective-permute-start(bf16[128,256]{1,0:T(8,128)(2,1)S(1)} %shard_map.99), channel_id=1, source_target_pairs={{0,20},{4,16},{8,28},{12,24},{16,4},{20,0},{24,12},{28,8},{1,21},{... | collective-permute-start | bytes 196616 | tf_op jit(solution)/shard_map/ppermute | solution.py:368
  32.1 8.7 %collective-permute-start.12 = (bf16[128,256]{1,0:T(8,128)(2,1)S(1)}, bf16[128,256]{1,0:T(8,128)(2,1)S(1)}, u32[]{:S(2)}, u32[]{:S(2)}) collective-permute-start(bf16[128,256]{1,0:T(8,128)(2,1)S(1)} %shard_map.100), channel_id=1, source_target_pairs={{0,4},{4,0},{8,12},{12,8},{16,20},{20,16},{24,28},{28,24},{1,5},{5... | collective-permute-start | bytes 196616 | tf_op jit(solution)/shard_map/ppermute | solution.py:368
  32.6 8.2 %collective-permute-start.13 = (bf16[128,256]{1,0:T(8,128)(2,1)S(1)}, bf16[128,256]{1,0:T(8,128)(2,1)S(1)}, u32[]{:S(2)}, u32[]{:S(2)}) collective-permute-start(bf16[128,256]{1,0:T(8,128)(2,1)S(1)} %shard_map.101), channel_id=1, source_target_pairs={{0,24},{4,28},{8,16},{12,20},{16,8},{20,12},{24,0},{28,4},{1,25},{... | collective-permute-start | bytes 196616 | tf_op jit(solution)/shard_map/ppermute | solution.py:368
  35.0 5.8 %collective-permute-start.14 = (bf16[128,256]{1,0:T(8,128)(2,1)S(1)}, bf16[128,256]{1,0:T(8,128)(2,1)S(1)}, u32[]{:S(2)}, u32[]{:S(2)}) collective-permute-start(bf16[128,256]{1,0:T(8,128)(2,1)S(1)} %shard_map.102), channel_id=1, source_target_pairs={{0,8},{4,12},{8,0},{12,4},{16,24},{20,28},{24,16},{28,20},{1,9},{5... | collective-permute-start | bytes 196616 | tf_op jit(solution)/shard_map/ppermute | solution.py:368
  37.1 7.0 %collective-permute-start.18 = (bf16[128,256]{1,0:T(8,128)(2,1)S(1)}, bf16[128,256]{1,0:T(8,128)(2,1)S(1)}, u32[]{:S(2)}, u32[]{:S(2)}) collective-permute-start(bf16[128,256]{1,0:T(8,128)(2,1)S(1)} %shard_map.104), channel_id=1, source_target_pairs={{0,28},{4,24},{8,20},{12,16},{16,12},{20,8},{24,4},{28,0},{1,29},{... | collective-permute-start | bytes 196616 | tf_op jit(solution)/shard_map/ppermute | solution.py:368
  40.8 5.2 %collective-permute-start.19 = (bf16[128,256]{1,0:T(8,128)(2,1)S(1)}, bf16[128,256]{1,0:T(8,128)(2,1)S(1)}, u32[]{:S(2)}, u32[]{:S(2)}) collective-permute-start(bf16[128,256]{1,0:T(8,128)(2,1)S(1)} %shard_map.105), channel_id=1, source_target_pairs={{0,12},{4,8},{8,4},{12,0},{16,28},{20,24},{24,20},{28,16},{1,13},{... | collective-permute-start | bytes 196616 | tf_op jit(solution)/shard_map/ppermute | solution.py:368

commit v2 on v1

--- a/solution.py
+++ b/solution.py
@@ -44,10 +44,16 @@
 def sequence(n):
     top = [k for k in range(1, n) if 2 * k >= n]
     low = [k for k in range(1, n) if 2 * k < n]
-    mixed = top[:1]
+    parts, cots = top[:1], top[:1]
     for i in range(len(low)):
-        mixed += [top[i + 1], low[i]]
-    return [("part", k) for k in mixed] + [("cot", k) for k in mixed]
+        parts += [top[i + 1], low[i]]
+        cots += [top[i + 1], low[i]] if i else [low[i], top[i + 1]]
+    return [("part", k) for k in parts] + [("cot", k) for k in cots]
+
+
+def batches(n):
+    order = [k for kind, k in sequence(n) if kind == "cot"]
+    return [order[:1]] + [order[i : i + 2] for i in range(1, len(order), 2)]
 
 
 def split_body(count, rows, wide_ref, *refs):
@@ -170,9 +176,11 @@
     return jnp.max(jnp.where(low, 0.0, mark)).astype(jnp.int32) * 128 + units
 
 
-def pick_body(bags, grad_ref, message_ref, out_ref):
-    tile = read_mark(message_ref, bags)
-    out_ref[...] = grad_ref[pl.ds(pl.multiple_of(tile * bags, bags), bags), :]
+def pick_body(bags, grad_ref, *refs):
+    half = len(refs) // 2
+    for message_ref, out_ref in zip(refs[:half], refs[half:], strict=True):
+        tile = read_mark(message_ref, bags)
+        out_ref[...] = grad_ref[pl.ds(pl.multiple_of(tile * bags, bags), bags), :]
 
 
 def own_tile(plan_ref):
@@ -356,22 +364,23 @@
     for kind, k in sequence(tables):
         if kind == "part":
             arrived[k] = lax.ppermute(blocks[k - 1], "table", pairs_of(k, tables))
-        else:
-            picked = call(
-                functools.partial(pick_body, bags),
-                near((bags, width), bf16),
-                [VMEM, VMEM],
-                VMEM,
-                (pooled_grad, arrived[k]),
-                limit=8 * mega,
-            )
-            returned[k] = lax.ppermute(picked, "table", pairs_of(k, tables))
+    for ks in batches(tables):
+        picked = call(
+            functools.partial(pick_body, bags),
+            [near((bags, width), bf16)] * len(ks),
+            [VMEM] * (1 + len(ks)),
+            [VMEM] * len(ks),
+            (pooled_grad, *[arrived[k] for k in ks]),
+            limit=8 * mega,
+        )
+        for k, block in zip(ks, picked, strict=True):
+            returned[k] = lax.ppermute(block, "table", pairs_of(k, tables))
 
     cut = max(len(returned) - LATE, 0)
     ahead, late = list(returned)[:cut], list(returned)[cut:]
     pooled, *turned, so_far, counts_late = call(
         functools.partial(
-            finish_body, ahead, late, min(512, rows), cols
+            finish_body, ahead, late, rows, cols
         ),
         [shape(pooled_grad.shape, bf16)]
         + [near((rows, width), bf16)] * 2

time: 47.9 us -> 46.4 us (0.969)
  waiting for transfers between devices: 9.24 us -> 5.09 us
  starting transfers between devices: 27.2 us -> 30.1 us
    ppermute x7, starting transfers between devices: 9.22 us -> 11.9 us  [per_device(): returned[k] = lax.ppermute(block, 'table', pairs_of(k, tables))]
    ppermute x7, waiting for transfers between devices: 6.04 us -> 3.78 us  [per_device(): returned[k] = lax.ppermute(block, 'table', pairs_of(k, tables))]
    ppermute x7, waiting for transfers between devices: 1.9 us -> 0.02 us  [per_device(): arrived[k] = lax.ppermute(blocks[k - 1], 'table', pairs_of(k, tables))]
    pallas_call x13 -> x10, Pallas kernels: 10.4 us -> 10.2 us  [call(): pl.pallas_call(body, out_shape=out_shape, in_specs=in_specs, out_specs=ou...]
  transfers between devices with their start and end apart: 20 -> 20, of which waited for: 6 -> 3; matrix products, arithmetic and copies ran while one was open for 0% -> 0% of each run, Pallas kernels for 16% -> 16%
where the time goes in v2:
time: 46.4 us; the launch traced here: 46.2 us
  starting transfers between devices  30.1 us (65%)
  Pallas kernels  10.2 us (22%)
  waiting for transfers between devices  5.09 us (11%)
  between operations  0.76 us (2%)
    ppermute x7, starting transfers between devices, per_device(): returned[k] = lax.ppermute(block, 'table', pairs_of(k, tables))  11.9 us
    ppermute x7, starting transfers between devices, per_device(): arrived[k] = lax.ppermute(blocks[k - 1], 'table', pairs_of(k, tables))  11.6 us
    pallas_call x10, Pallas kernels, call(): pl.pallas_call(body, out_shape=out_shape, in_specs=in_specs, out_specs=ou...  10.2 us
    ppermute x6, starting transfers between devices, over_col(): lax.ppermute(parts[k], 'col', pairs_of(k, cols))  6.52 us
    ppermute x7, waiting for transfers between devices, per_device(): returned[k] = lax.ppermute(block, 'table', pairs_of(k, tables))  3.78 us
    ppermute x6, waiting for transfers between devices, over_col(): lax.ppermute(parts[k], 'col', pairs_of(k, cols))  1.3 us
  transfers between devices with their start and end apart: 20, of which 3 were waited for; matrix products, arithmetic and copies ran while one was open for 0% of the time, Pallas kernels for 16%

profile of v2, /device:TPU:0, one launch (start us, length us, event | category | flops | bytes accessed | tf_op | source)
XLA Modules:
  0.0 46.2 jit_solution(375310376077979675)
XLA Ops:
  0.6 1.1 %shard_map.95 = (bf16[64,1024]{1,0:T(8,128)(2,1)S(1)}, bf16[64,1024]{1,0:T(8,128)(2,1)S(1)}, bf16[64,1024]{1,0:T(8,128)(2,1)S(1)}, bf16[64,1024]{1,0:T(8,128)(2,1)S(1)}) custom-call(bf16[64,4096]{1,0:T(8,128)(2,1)} %bitcast.4), custom_call_target="tpu_custom_call" | custom-call | bytes 524288 | tf_op jit(solution)/shard_map/pallas_call | solution.py:29
  1.8 0.6 %collective-permute-start = (bf16[64,1024]{1,0:T(8,128)(2,1)S(1)}, bf16[64,1024]{1,0:T(8,128)(2,1)S(1)}, u32[]{:S(2)}, u32[]{:S(2)}) collective-permute-start(bf16[64,1024]{1,0:T(8,128)(2,1)S(1)} %get-tuple-element.37), channel_id=1, source_target_pairs={{0,1},{1,0},{2,3},{3,2},{4,5},{5,4},{6,7},{7,6},{8,9},{9,8},{10,11... | collective-permute-start | bytes 393224 | tf_op jit(solution)/shard_map/ppermute | solution.py:301
  2.3 2.6 %collective-permute-start.1 = (bf16[64,1024]{1,0:T(8,128)(2,1)S(1)}, bf16[64,1024]{1,0:T(8,128)(2,1)S(1)}, u32[]{:S(2)}, u32[]{:S(2)}) collective-permute-start(bf16[64,1024]{1,0:T(8,128)(2,1)S(1)} %get-tuple-element.38), channel_id=1, source_target_pairs={{0,2},{1,3},{2,0},{3,1},{4,6},{5,7},{6,4},{7,5},{8,10},{9,11},{10,... | collective-permute-start | bytes 393224 | tf_op jit(solution)/shard_map/ppermute | solution.py:301
  4.9 0.0 collective-permute-start.2
  4.9 2.7 %shard_map.94 = (bf16[1024,1024]{1,0:T(8,128)(2,1)S(1)}, s32[2,8]{1,0:T(2,128)S(1)}, bf16[64,1024]{1,0:T(8,128)(2,1)S(1)}, bf16[64,1024]{1,0:T(8,128)(2,1)S(1)},...) custom-call(f32[64,4096]{1,0:T(8,128)} %bitcast.3, s32[8,4,128]{2,1,0:T(4,128)} %bitcast.5, ...), custom_call_target="tpu_custom_call" | custom-call | bytes 1069120 | tf_op jit(solution)/shard_map/pallas_call | solution.py:29
  7.6 0.2 collective-permute-start.15
  7.8 1.9 %collective-permute-start.16 = (bf16[64,1024]{1,0:T(8,128)(2,1)S(1)}, bf16[64,1024]{1,0:T(8,128)(2,1)S(1)}, u32[]{:S(2)}, u32[]{:S(2)}) collective-permute-start(bf16[64,1024]{1,0:T(8,128)(2,1)S(1)} %get-tuple-element.54), channel_id=1, source_target_pairs={{0,2},{1,3},{2,0},{3,1},{4,6},{5,7},{6,4},{7,5},{8,10},{9,11},{10,... | collective-permute-start | bytes 393224 | tf_op jit(solution)/shard_map/ppermute | solution.py:301
  9.8 0.5 %shard_map.96.early_ref = bf16[8,128,128]{2,1,0:T(8,128)(2,1)S(1)} custom-call(bf16[1024,1024]{1,0:T(8,128)(2,1)S(1)} %get-tuple-element.35.counts_ref, bf16[64,1024]{1,0:T(8,128)(2,1)S(1)} %get-tuple-element.36.refs_0_.refs_12_, bf16[64,1024]{1,0:T(8,128)(2,1)S(1)} %collective-permute-done.refs_1_.refs_13_), custom_call_target="tpu_custom_call" | custom-call | flops 268435456 | bytes 2359296 | tf_op jit(solution)/shard_map/pallas_call | solution.py:29
  10.3 1.3 %collective-permute-done.2.refs_1_.refs_15_ = bf16[64,1024]{1,0:T(8,128)(2,1)S(1)} collective-permute-done((bf16[64,1024]{1,0:T(8,128)(2,1)S(1)}, bf16[64,1024]{1,0:T(8,128)(2,1)S(1)}, u32[]{:S(2)}, u32[]{:S(2)}) %collective-permute-start.2) | collective-permute-done | bytes 131104 | tf_op jit(solution)/shard_map/ppermute | solution.py:301
  11.6 1.1 %shard_map.97 = (bf16[256,128]{1,0:T(8,128)(2,1)S(1)}, bf16[264,128]{1,0:T(8,128)(2,1)S(1)}, bf16[264,128]{1,0:T(8,128)(2,1)S(1)}, bf16[264,128]{1,0:T(8,128)(2,...) custom-call(s32[2,8]{1,0:T(2,128)S(1)} %get-tuple-element.34.plan_re, ...), custom_call_target="tpu_custom_call" | custom-call | flops 268435456 | bytes 2621504 | tf_op jit(solution)/shard_map/pallas_call | solution.py:29
  12.7 3.7 %collective-permute-start.6 = (bf16[264,128]{1,0:T(8,128)(2,1)S(1)}, bf16[264,128]{1,0:T(8,128)(2,1)S(1)}, u32[]{:S(2)}, u32[]{:S(2)}) collective-permute-start(bf16[264,128]{1,0:T(8,128)(2,1)S(1)} %get-tuple-element.44), channel_id=1, source_target_pairs={{0,24},{4,28},{8,16},{12,20},{16,8},{20,12},{24,0},{28,4},{1,25},{... | collective-permute-start | bytes 202760 | tf_op jit(solution)/shard_map/ppermute | solution.py:366
  16.4 1.7 %collective-permute-start.4 = (bf16[264,128]{1,0:T(8,128)(2,1)S(1)}, bf16[264,128]{1,0:T(8,128)(2,1)S(1)}, u32[]{:S(2)}, u32[]{:S(2)}) collective-permute-start(bf16[264,128]{1,0:T(8,128)(2,1)S(1)} %get-tuple-element.42), channel_id=1, source_target_pairs={{0,20},{4,16},{8,28},{12,24},{16,4},{20,0},{24,12},{28,8},{1,21},{... | collective-permute-start | bytes 202760 | tf_op jit(solution)/shard_map/ppermute | solution.py:366
  18.1 1.2 %collective-permute-start.17 = (bf16[64,1024]{1,0:T(8,128)(2,1)S(1)}, bf16[64,1024]{1,0:T(8,128)(2,1)S(1)}, u32[]{:S(2)}, u32[]{:S(2)}) collective-permute-start(bf16[64,1024]{1,0:T(8,128)(2,1)S(1)} %get-tuple-element.55), channel_id=1, source_target_pairs={{0,3},{1,2},{2,1},{3,0},{4,7},{5,6},{6,5},{7,4},{8,11},{9,10},{10,... | collective-permute-start | bytes 393224 | tf_op jit(solution)/shard_map/ppermute | solution.py:301
  19.3 0.5 %collective-permute-start.5 = (bf16[264,128]{1,0:T(8,128)(2,1)S(1)}, bf16[264,128]{1,0:T(8,128)(2,1)S(1)}, u32[]{:S(2)}, u32[]{:S(2)}) collective-permute-start(bf16[264,128]{1,0:T(8,128)(2,1)S(1)} %get-tuple-element.43), channel_id=1, source_target_pairs={{0,4},{4,0},{8,12},{12,8},{16,20},{20,16},{24,28},{28,24},{1,5},{5... | collective-permute-start | bytes 202760 | tf_op jit(solution)/shard_map/ppermute | solution.py:366
  19.8 2.3 %collective-permute-start.3 = (bf16[264,128]{1,0:T(8,128)(2,1)S(1)}, bf16[264,128]{1,0:T(8,128)(2,1)S(1)}, u32[]{:S(2)}, u32[]{:S(2)}) collective-permute-start(bf16[264,128]{1,0:T(8,128)(2,1)S(1)} %get-tuple-element.41), channel_id=1, source_target_pairs={{0,16},{4,20},{8,24},{12,28},{16,0},{20,4},{24,8},{28,12},{1,17},{... | collective-permute-start | bytes 202760 | tf_op jit(solution)/shard_map/ppermute | solution.py:366
  22.1 2.2 %collective-permute-start.8 = (bf16[264,128]{1,0:T(8,128)(2,1)S(1)}, bf16[264,128]{1,0:T(8,128)(2,1)S(1)}, u32[]{:S(2)}, u32[]{:S(2)}) collective-permute-start(bf16[264,128]{1,0:T(8,128)(2,1)S(1)} %get-tuple-element.46), channel_id=1, source_target_pairs={{0,28},{4,24},{8,20},{12,16},{16,12},{20,8},{24,4},{28,0},{1,29},{... | collective-permute-start | bytes 202760 | tf_op jit(solution)/shard_map/ppermute | solution.py:366
  24.3 1.2 %collective-permute-start.9 = (bf16[264,128]{1,0:T(8,128)(2,1)S(1)}, bf16[264,128]{1,0:T(8,128)(2,1)S(1)}, u32[]{:S(2)}, u32[]{:S(2)}) collective-permute-start(bf16[264,128]{1,0:T(8,128)(2,1)S(1)} %get-tuple-element.47), channel_id=1, source_target_pairs={{0,12},{4,8},{8,4},{12,0},{16,28},{20,24},{24,20},{28,16},{1,13},{... | collective-permute-start | bytes 202760 | tf_op jit(solution)/shard_map/ppermute | solution.py:366
  25.5 0.1 shard_map.100
  25.7 2.2 %collective-permute-start.13 = (bf16[128,256]{1,0:T(8,128)(2,1)S(1)}, bf16[128,256]{1,0:T(8,128)(2,1)S(1)}, u32[]{:S(2)}, u32[]{:S(2)}) collective-permute-start(bf16[128,256]{1,0:T(8,128)(2,1)S(1)} %get-tuple-element.50), channel_id=1, source_target_pairs={{0,24},{4,28},{8,16},{12,20},{16,8},{20,12},{24,0},{28,4},{1,25},{... | collective-permute-start | bytes 196616 | tf_op jit(solution)/shard_map/ppermute | solution.py:377
  27.9 0.5 collective-permute-start.14
  28.4 0.1 shard_map.98
  28.5 0.1 shard_map.99
  28.7 1.7 %collective-permute-start.11 = (bf16[128,256]{1,0:T(8,128)(2,1)S(1)}, bf16[128,256]{1,0:T(8,128)(2,1)S(1)}, u32[]{:S(2)}, u32[]{:S(2)}) collective-permute-start(bf16[128,256]{1,0:T(8,128)(2,1)S(1)} %get-tuple-element.48), channel_id=1, source_target_pairs={{0,4},{4,0},{8,12},{12,8},{16,20},{20,16},{24,28},{28,24},{1,5},{5... | collective-permute-start | bytes 196616 | tf_op jit(solution)/shard_map/ppermute | solution.py:377
  30.4 3.1 %collective-permute-start.12 = (bf16[128,256]{1,0:T(8,128)(2,1)S(1)}, bf16[128,256]{1,0:T(8,128)(2,1)S(1)}, u32[]{:S(2)}, u32[]{:S(2)}) collective-permute-start(bf16[128,256]{1,0:T(8,128)(2,1)S(1)} %get-tuple-element.49), channel_id=1, source_target_pairs={{0,20},{4,16},{8,28},{12,24},{16,4},{20,0},{24,12},{28,8},{1,21},{... | collective-permute-start | bytes 196616 | tf_op jit(solution)/shard_map/ppermute | solution.py:377
  33.5 0.3 collective-permute-start.10
  33.8 0.1 shard_map.102
  34.0 3.1 %collective-permute-start.18 = (bf16[128,256]{1,0:T(8,128)(2,1)S(1)}, bf16[128,256]{1,0:T(8,128)(2,1)S(1)}, u32[]{:S(2)}, u32[]{:S(2)}) collective-permute-start(bf16[128,256]{1,0:T(8,128)(2,1)S(1)} %get-tuple-element.61), channel_id=1, source_target_pairs={{0,28},{4,24},{8,20},{12,16},{16,12},{20,8},{24,4},{28,0},{1,29},{... | collective-permute-start | bytes 196616 | tf_op jit(solution)/shard_map/ppermute | solution.py:377
  37.0 1.1 %collective-permute-start.19 = (bf16[128,256]{1,0:T(8,128)(2,1)S(1)}, bf16[128,256]{1,0:T(8,128)(2,1)S(1)}, u32[]{:S(2)}, u32[]{:S(2)}) collective-permute-start(bf16[128,256]{1,0:T(8,128)(2,1)S(1)} %get-tuple-element.62), channel_id=1, source_target_pairs={{0,12},{4,8},{8,4},{12,0},{16,28},{20,24},{24,20},{28,16},{1,13},{... | collective-permute-start | bytes 196616 | tf_op jit(solution)/shard_map/ppermute | solution.py:377
  38.1 1.0 %collective-permute-done.12.refs_9_ = bf16[128,256]{1,0:T(8,128)(2,1)S(1)} collective-permute-done((bf16[128,256]{1,0:T(8,128)(2,1)S(1)}, bf16[128,256]{1,0:T(8,128)(2,1)S(1)}, u32[]{:S(2)}, u32[]{:S(2)}) %collective-permute-start.12) | collective-permute-done | bytes 65568 | tf_op jit(solution)/shard_map/ppermute | solution.py:377
  39.1 2.7 %collective-permute-done.10.refs_7_ = bf16[128,256]{1,0:T(8,128)(2,1)S(1)} collective-permute-done((bf16[128,256]{1,0:T(8,128)(2,1)S(1)}, bf16[128,256]{1,0:T(8,128)(2,1)S(1)}, u32[]{:S(2)}, u32[]{:S(2)}) %collective-permute-start.10) | collective-permute-done | bytes 65568 | tf_op jit(solution)/shard_map/ppermute | solution.py:377
  41.9 2.6 %shard_map.101 = (bf16[2048,256]{1,0:T(8,128)(2,1)}, bf16[1024,256]{1,0:T(8,128)(2,1)S(1)}, bf16[1024,256]{1,0:T(8,128)(2,1)S(1)}, f32[1024,256]{1,0:T(8,128)S(1)}, bf16[1024,256]{1,0:T(8,128)(2,1)S(1)}) custom-call(s32[2,8]{1,0:T(2,128)S(1)} %get-tuple-element.34.plan_ref, bf16[256,128]{1,0:T(8,128)(2,1)S(1)} %get-tuple-element.40.own_ref, ...), custom_call_target="tpu_custom_call" | custom-call | flops 536870912 | bytes 5060672 | tf_op jit(solution)/shard_map/pallas_call | solution.py:29
  44.5 1.7 %shard_map.103 = (bf16[1024,256]{1,0:T(8,128)(2,1)}, f32[1024,256]{1,0:T(8,128)}) custom-call(f32[1024,256]{1,0:T(8,128)S(1)} %get-tuple-element.57.sum_ref, bf16[1024,256]{1,0:T(8,128)(2,1)S(1)} %get-tuple-element.58.counts_ref, bf16[1024,256]{1,0:T(8,128)(2,1)S(1)} %get-tuple-element.59.rows_ref, bf16[1024,256]{1,0:T(8,128)(2,1)S(1)} %get-tuple-element.60.state_ref, ...), custom_call_target="tpu_custom_call" | custom-call | flops 134217728 | bytes 2752512 | tf_op jit(solution)/shard_map/pallas_call | solution.py:29
  (20 shorter events, 0.1 us)
Async XLA Ops:
  1.8 8.0 %collective-permute-start = (bf16[64,1024]{1,0:T(8,128)(2,1)S(1)}, bf16[64,1024]{1,0:T(8,128)(2,1)S(1)}, u32[]{:S(2)}, u32[]{:S(2)}) collective-permute-start(bf16[64,1024]{1,0:T(8,128)(2,1)S(1)} %get-tuple-element.37), channel_id=1, source_target_pairs={{0,1},{1,0},{2,3},{3,2},{4,5},{5,4},{6,7},{7,6},{8,9},{9,8},{10,11... | collective-permute-start | bytes 393224 | tf_op jit(solution)/shard_map/ppermute | solution.py:301
  2.3 8.0 %collective-permute-start.1 = (bf16[64,1024]{1,0:T(8,128)(2,1)S(1)}, bf16[64,1024]{1,0:T(8,128)(2,1)S(1)}, u32[]{:S(2)}, u32[]{:S(2)}) collective-permute-start(bf16[64,1024]{1,0:T(8,128)(2,1)S(1)} %get-tuple-element.38), channel_id=1, source_target_pairs={{0,2},{1,3},{2,0},{3,1},{4,6},{5,7},{6,4},{7,5},{8,10},{9,11},{10,... | collective-permute-start | bytes 393224 | tf_op jit(solution)/shard_map/ppermute | solution.py:301
  4.9 6.7 %collective-permute-start.2 = (bf16[64,1024]{1,0:T(8,128)(2,1)S(1)}, bf16[64,1024]{1,0:T(8,128)(2,1)S(1)}, u32[]{:S(2)}, u32[]{:S(2)}) collective-permute-start(bf16[64,1024]{1,0:T(8,128)(2,1)S(1)} %get-tuple-element.39), channel_id=1, source_target_pairs={{0,3},{1,2},{2,1},{3,0},{4,7},{5,6},{6,5},{7,4},{8,11},{9,10},{10,... | collective-permute-start | bytes 393224 | tf_op jit(solution)/shard_map/ppermute | solution.py:301
  7.6 10.5 %collective-permute-start.15 = (bf16[64,1024]{1,0:T(8,128)(2,1)S(1)}, bf16[64,1024]{1,0:T(8,128)(2,1)S(1)}, u32[]{:S(2)}, u32[]{:S(2)}) collective-permute-start(bf16[64,1024]{1,0:T(8,128)(2,1)S(1)} %get-tuple-element.53), channel_id=1, source_target_pairs={{0,1},{1,0},{2,3},{3,2},{4,5},{5,4},{6,7},{7,6},{8,9},{9,8},{10,11... | collective-permute-start | bytes 393224 | tf_op jit(solution)/shard_map/ppermute | solution.py:301
  7.8 11.5 %collective-permute-start.16 = (bf16[64,1024]{1,0:T(8,128)(2,1)S(1)}, bf16[64,1024]{1,0:T(8,128)(2,1)S(1)}, u32[]{:S(2)}, u32[]{:S(2)}) collective-permute-start(bf16[64,1024]{1,0:T(8,128)(2,1)S(1)} %get-tuple-element.54), channel_id=1, source_target_pairs={{0,2},{1,3},{2,0},{3,1},{4,6},{5,7},{6,4},{7,5},{8,10},{9,11},{10,... | collective-permute-start | bytes 393224 | tf_op jit(solution)/shard_map/ppermute | solution.py:301
  9.8 15.8 %copy-start = (bf16[2048,256]{1,0:T(8,128)(2,1)S(1)}, bf16[2048,256]{1,0:T(8,128)(2,1)}, u32[]{:S(2)}) copy-start(bf16[2048,256]{1,0:T(8,128)(2,1)} %grad_ref.9) | copy-start | bytes 3145732
  12.7 7.1 %collective-permute-start.6 = (bf16[264,128]{1,0:T(8,128)(2,1)S(1)}, bf16[264,128]{1,0:T(8,128)(2,1)S(1)}, u32[]{:S(2)}, u32[]{:S(2)}) collective-permute-start(bf16[264,128]{1,0:T(8,128)(2,1)S(1)} %get-tuple-element.44), channel_id=1, source_target_pairs={{0,24},{4,28},{8,16},{12,20},{16,8},{20,12},{24,0},{28,4},{1,25},{... | collective-permute-start | bytes 202760 | tf_op jit(solution)/shard_map/ppermute | solution.py:366
  16.4 5.8 %collective-permute-start.7 = (bf16[264,128]{1,0:T(8,128)(2,1)S(1)}, bf16[264,128]{1,0:T(8,128)(2,1)S(1)}, u32[]{:S(2)}, u32[]{:S(2)}) collective-permute-start(bf16[264,128]{1,0:T(8,128)(2,1)S(1)} %get-tuple-element.45), channel_id=1, source_target_pairs={{0,8},{4,12},{8,0},{12,4},{16,24},{20,28},{24,16},{28,20},{1,9},{5... | collective-permute-start | bytes 202760 | tf_op jit(solution)/shard_map/ppermute | solution.py:366
  16.4 8.0 %collective-permute-start.4 = (bf16[264,128]{1,0:T(8,128)(2,1)S(1)}, bf16[264,128]{1,0:T(8,128)(2,1)S(1)}, u32[]{:S(2)}, u32[]{:S(2)}) collective-permute-start(bf16[264,128]{1,0:T(8,128)(2,1)S(1)} %get-tuple-element.42), channel_id=1, source_target_pairs={{0,20},{4,16},{8,28},{12,24},{16,4},{20,0},{24,12},{28,8},{1,21},{... | collective-permute-start | bytes 202760 | tf_op jit(solution)/shard_map/ppermute | solution.py:366
  18.1 10.5 %collective-permute-start.17 = (bf16[64,1024]{1,0:T(8,128)(2,1)S(1)}, bf16[64,1024]{1,0:T(8,128)(2,1)S(1)}, u32[]{:S(2)}, u32[]{:S(2)}) collective-permute-start(bf16[64,1024]{1,0:T(8,128)(2,1)S(1)} %get-tuple-element.55), channel_id=1, source_target_pairs={{0,3},{1,2},{2,1},{3,0},{4,7},{5,6},{6,5},{7,4},{8,11},{9,10},{10,... | collective-permute-start | bytes 393224 | tf_op jit(solution)/shard_map/ppermute | solution.py:301
  19.3 6.4 %collective-permute-start.5 = (bf16[264,128]{1,0:T(8,128)(2,1)S(1)}, bf16[264,128]{1,0:T(8,128)(2,1)S(1)}, u32[]{:S(2)}, u32[]{:S(2)}) collective-permute-start(bf16[264,128]{1,0:T(8,128)(2,1)S(1)} %get-tuple-element.43), channel_id=1, source_target_pairs={{0,4},{4,0},{8,12},{12,8},{16,20},{20,16},{24,28},{28,24},{1,5},{5... | collective-permute-start | bytes 202760 | tf_op jit(solution)/shard_map/ppermute | solution.py:366
  19.8 8.1 %collective-permute-start.3 = (bf16[264,128]{1,0:T(8,128)(2,1)S(1)}, bf16[264,128]{1,0:T(8,128)(2,1)S(1)}, u32[]{:S(2)}, u32[]{:S(2)}) collective-permute-start(bf16[264,128]{1,0:T(8,128)(2,1)S(1)} %get-tuple-element.41), channel_id=1, source_target_pairs={{0,16},{4,20},{8,24},{12,28},{16,0},{20,4},{24,8},{28,12},{1,17},{... | collective-permute-start | bytes 202760 | tf_op jit(solution)/shard_map/ppermute | solution.py:366
  22.1 8.3 %collective-permute-start.8 = (bf16[264,128]{1,0:T(8,128)(2,1)S(1)}, bf16[264,128]{1,0:T(8,128)(2,1)S(1)}, u32[]{:S(2)}, u32[]{:S(2)}) collective-permute-start(bf16[264,128]{1,0:T(8,128)(2,1)S(1)} %get-tuple-element.46), channel_id=1, source_target_pairs={{0,28},{4,24},{8,20},{12,16},{16,12},{20,8},{24,4},{28,0},{1,29},{... | collective-permute-start | bytes 202760 | tf_op jit(solution)/shard_map/ppermute | solution.py:366
  24.3 9.2 %collective-permute-start.9 = (bf16[264,128]{1,0:T(8,128)(2,1)S(1)}, bf16[264,128]{1,0:T(8,128)(2,1)S(1)}, u32[]{:S(2)}, u32[]{:S(2)}) collective-permute-start(bf16[264,128]{1,0:T(8,128)(2,1)S(1)} %get-tuple-element.47), channel_id=1, source_target_pairs={{0,12},{4,8},{8,4},{12,0},{16,28},{20,24},{24,20},{28,16},{1,13},{... | collective-permute-start | bytes 202760 | tf_op jit(solution)/shard_map/ppermute | solution.py:366
  25.7 8.2 %collective-permute-start.13 = (bf16[128,256]{1,0:T(8,128)(2,1)S(1)}, bf16[128,256]{1,0:T(8,128)(2,1)S(1)}, u32[]{:S(2)}, u32[]{:S(2)}) collective-permute-start(bf16[128,256]{1,0:T(8,128)(2,1)S(1)} %get-tuple-element.50), channel_id=1, source_target_pairs={{0,24},{4,28},{8,16},{12,20},{16,8},{20,12},{24,0},{28,4},{1,25},{... | collective-permute-start | bytes 196616 | tf_op jit(solution)/shard_map/ppermute | solution.py:377
  27.9 9.1 %collective-permute-start.14 = (bf16[128,256]{1,0:T(8,128)(2,1)S(1)}, bf16[128,256]{1,0:T(8,128)(2,1)S(1)}, u32[]{:S(2)}, u32[]{:S(2)}) collective-permute-start(bf16[128,256]{1,0:T(8,128)(2,1)S(1)} %get-tuple-element.51), channel_id=1, source_target_pairs={{0,8},{4,12},{8,0},{12,4},{16,24},{20,28},{24,16},{28,20},{1,9},{5... | collective-permute-start | bytes 196616 | tf_op jit(solution)/shard_map/ppermute | solution.py:377
  28.7 9.4 %collective-permute-start.11 = (bf16[128,256]{1,0:T(8,128)(2,1)S(1)}, bf16[128,256]{1,0:T(8,128)(2,1)S(1)}, u32[]{:S(2)}, u32[]{:S(2)}) collective-permute-start(bf16[128,256]{1,0:T(8,128)(2,1)S(1)} %get-tuple-element.48), channel_id=1, source_target_pairs={{0,4},{4,0},{8,12},{12,8},{16,20},{20,16},{24,28},{28,24},{1,5},{5... | collective-permute-start | bytes 196616 | tf_op jit(solution)/shard_map/ppermute | solution.py:377
  30.4 8.7 %collective-permute-start.12 = (bf16[128,256]{1,0:T(8,128)(2,1)S(1)}, bf16[128,256]{1,0:T(8,128)(2,1)S(1)}, u32[]{:S(2)}, u32[]{:S(2)}) collective-permute-start(bf16[128,256]{1,0:T(8,128)(2,1)S(1)} %get-tuple-element.49), channel_id=1, source_target_pairs={{0,20},{4,16},{8,28},{12,24},{16,4},{20,0},{24,12},{28,8},{1,21},{... | collective-permute-start | bytes 196616 | tf_op jit(solution)/shard_map/ppermute | solution.py:377
  33.5 8.4 %collective-permute-start.10 = (bf16[128,256]{1,0:T(8,128)(2,1)S(1)}, bf16[128,256]{1,0:T(8,128)(2,1)S(1)}, u32[]{:S(2)}, u32[]{:S(2)}) collective-permute-start(bf16[128,256]{1,0:T(8,128)(2,1)S(1)} %shard_map.98), channel_id=1, source_target_pairs={{0,16},{4,20},{8,24},{12,28},{16,0},{20,4},{24,8},{28,12},{1,17},{... | collective-permute-start | bytes 196616 | tf_op jit(solution)/shard_map/ppermute | solution.py:377
  34.0 10.5 %collective-permute-start.18 = (bf16[128,256]{1,0:T(8,128)(2,1)S(1)}, bf16[128,256]{1,0:T(8,128)(2,1)S(1)}, u32[]{:S(2)}, u32[]{:S(2)}) collective-permute-start(bf16[128,256]{1,0:T(8,128)(2,1)S(1)} %get-tuple-element.61), channel_id=1, source_target_pairs={{0,28},{4,24},{8,20},{12,16},{16,12},{20,8},{24,4},{28,0},{1,29},{... | collective-permute-start | bytes 196616 | tf_op jit(solution)/shard_map/ppermute | solution.py:377
  37.0 7.4 %collective-permute-start.19 = (bf16[128,256]{1,0:T(8,128)(2,1)S(1)}, bf16[128,256]{1,0:T(8,128)(2,1)S(1)}, u32[]{:S(2)}, u32[]{:S(2)}) collective-permute-start(bf16[128,256]{1,0:T(8,128)(2,1)S(1)} %get-tuple-element.62), channel_id=1, source_target_pairs={{0,12},{4,8},{8,4},{12,0},{16,28},{20,24},{24,20},{28,16},{1,13},{... | collective-permute-start | bytes 196616 | tf_op jit(solution)/shard_map/ppermute | solution.py:377
